TPU v7x, 32 devices: a whole 2x2x4 slice. The times are simulated.
32 devices in a mesh: snap: 2 (over x), row: 16 (over z, y, core).
Axes of the slice: x: 2, y: 2, z: 4, core: 2. Of those that a mesh axis runs over, the one named last changes fastest.
Arguments:
- snapshots: bfloat16 [256, 262144], P('snap', 'row'), may hold values from -64 to 64
- counts: int32 [16], P('row'), may hold values from 1 to 16384, 196608 in all
Outputs:
- basis: bfloat16 [256, 262144], P('snap', 'row')
- r_factor: float32 [256, 256], replicated
Inputs may be any that keep to these rules, and one draw needn't show every extreme that they name: `counts`: at least one row and at most 16384 rows are live on each index of row, and some index has all 16384 live.
All inputs are finite; a program needn't handle non-finite values. No bound on the sum of `counts` on one device may be relied on, other than what follows from the above.
Results may differ from a plain program's by a relative error of at most 0.0049.
Values may be sent and summed in bfloat16 or wider, within the bound.
A program may use at most 64 MiB of HBM per device.

v0:
```python
import math

import jax
import jax.numpy as jnp
from jax import lax
from jax.sharding import PartitionSpec as P


def gram_of(block):
    return lax.dot_general(
        block, block, (((1,), (1,)), ((), ())), preferred_element_type=jnp.float32
    )


def factors(gram, scale):
    lower = jnp.linalg.cholesky(gram)
    r_factor = lower.T / scale
    width = gram.shape[0]
    inverse = lax.linalg.triangular_solve(
        lower, jnp.eye(width, dtype=jnp.float32), left_side=True, lower=True
    ).T
    weights = (inverse * scale).astype(jnp.bfloat16)
    return (r_factor, weights)


def apply_weights(weights, block):
    return lax.dot_general(
        weights, block, (((0,), (0,)), ((), ())), preferred_element_type=jnp.float32
    ).astype(jnp.bfloat16)


def shards(snapshots, counts):
    narrow, slots = snapshots.shape
    slot = lax.broadcasted_iota(jnp.int32, (1, slots), 1)
    live = jnp.where(slot < counts[0], snapshots, jnp.zeros_like(snapshots))
    scale = math.sqrt(slots * lax.axis_size("row"))
    whole = lax.all_gather(live, "snap", axis=0, tiled=True)
    gram = lax.psum(gram_of(whole), "row")
    r_factor, weights = factors(gram, scale)
    start = lax.axis_index("snap") * narrow
    own_weights = lax.dynamic_slice_in_dim(weights, start, narrow, 1)
    basis = apply_weights(own_weights, whole)
    return (basis, r_factor)


def solution(mesh):
    placed = (P("snap", "row"), P("row"))
    return jax.shard_map(
        shards, mesh=mesh, in_specs=placed, out_specs=(P("snap", "row"), P()), check_vma=False
    )
```

profile of v0, /device:TPU:0, one launch (start us, length us, event | category | flops | bytes accessed | tf_op | source)
XLA Modules:
  0.0 294.9 jit_solution(8530265544125170200)
XLA Ops:
  7.9 4.8 %broadcast_select_fusion = bf16[128,16384]{1,0:T(8,128)(2,1)} fusion(bf16[128,16384]{1,0:T(8,128)(2,1)} %param.2, pred[16384]{0:T(1024)(128)(4,1)S(1)} %iota_compare_fusion.3), kind=kLoop, calls=%fused_computation.3 | loop fusion | flops 2097152 | bytes 8404992 | tf_op jit(solution)/shard_map/jit(_where)/select_n | solution.py:35
  12.7 106.8 %all-gather.2.cloned.1.call-done = bf16[256,16384]{1,0:T(8,128)(2,1)} async-done(((bf16[128,16384]{1,0:T(8,128)(2,1)}), bf16[256,16384]{1,0:T(8,128)(2,1)}) %all-gather.2.cloned.1.call-update) | async-done | bytes 8388624 | tf_op jit(solution)/shard_map/all_gather | solution.py:37
  119.5 8.8 %fusion.18 = f32[256,256]{0,1:T(8,128)} fusion(bf16[256,16384]{1,0:T(8,128)(2,1)} %all-gather.2.cloned.1.call-done), kind=kOutput, calls=%fused_computation.43 | convolution fusion | flops 2147483648 | bytes 8650752 | tf_op jit(solution)/shard_map/dot_general | solution.py:10
  128.5 89.8 %all-reduce.3.cloned.1.call-done = f32[256,256]{0,1:T(8,128)} async-done(((f32[256,256]{0,1:T(8,128)}), f32[256,256]{0,1:T(8,128)}) %all-reduce.3.cloned.1.call-update) | async-done | bytes 262160 | tf_op jit(solution)/shard_map/psum | solution.py:38
  218.2 1.1 copy.5
  219.3 1.0 fusion
  220.3 11.7 %cholesky.50 = f32[128,128]{1,0:T(8,128)S(1)} custom-call(f32[128,128]{1,0:T(8,128)S(1)} %cholesky.118), custom_call_target="Cholesky" | custom-call | tf_op jit(solution)/shard_map/jit(cholesky)/cholesky | solution.py:16
  232.1 9.8 %custom-call.14 = f32[1,128,128]{1,2,0:T(8,128)S(1)} custom-call(f32[1,128,128]{2,1,0:T(8,128)S(1)} %get-tuple-element.27), custom_call_target="InvertDiagBlocksLowerTriangular" | custom-call | tf_op jit(solution)/shard_map/jit(cholesky)/cholesky | solution.py:16
  241.9 0.2 constant_dynamic-update-slice_fusion
  242.1 0.3 convolution_subtract_fusion.1
  242.4 11.8 %cholesky.105 = f32[128,128]{1,0:T(8,128)S(1)} custom-call(f32[128,128]{1,0:T(8,128)S(1)} %convolution_subtract_fusion.1), custom_call_target="Cholesky" | custom-call | tf_op jit(solution)/shard_map/jit(cholesky)/cholesky | solution.py:16
  254.3 0.6 compare_reduce_fusion
  256.2 0.8 copy.6
  257.0 0.1 triangular_solve.63
  257.1 3.7 %while.1 = (s32[]{:T(128)}, f32[256,256]{1,0:T(8,128)S(1)}, s32[2,2]{1,0:T(2,128)S(1)}, f32[2,128,128]{2,1,0:T(8,128)S(1)}, s32[]{:T(128)}) while((s32[]{:T(128)}, f32[256,256]{1,0:T(8,128)S(1)}, s32[2,2]{1,0:T(2,128)S(1)}, f32[2,128,128]{2,1,0:T(8,128)S(1)}, s32[]{:T(128)}) %tuple.29), condition=%wide.while_cond, body=%wide.while_body.sunk | while | flops 2 | bytes 131189 | solution.py:19
  257.1 0.6 fusion.27
  257.6 1.3 bitcast_dynamic-update-slice_fusion.2
  259.0 0.6 fusion.27
  259.5 1.3 bitcast_dynamic-update-slice_fusion.2
  260.8 19.7 %custom-call.15 = f32[2,128,128]{1,2,0:T(8,128)S(1)} custom-call(f32[2,128,128]{2,1,0:T(8,128)S(1)} %get-tuple-element.9), custom_call_target="InvertDiagBlocksLowerTriangular" | custom-call | tf_op jit(solution)/shard_map/triangular_solve | solution.py:19
  280.5 0.3 fusion.5
  280.8 0.3 convolution_subtract_fusion
  281.0 0.3 fusion.10
  281.4 6.7 %convolution_convert_fusion = bf16[128,16384]{1,0:T(8,128)(2,1)} fusion(bf16[256,16384]{1,0:T(8,128)(2,1)} %all-gather.2.cloned.1.call-done, s32[]{:T(128)S(6)} %select_n.13, f32[128,256]{1,0:T(8,128)S(1)} %fusion.5, f32[128,256]{1,0:T(8,128)S(1)} %fusion.10), kind=kOutput, calls=%fused_computation.2 | convolution fusion | flops 1075937280 | bytes 12845060 | tf_op jit(solution)/shard_map/dot_general | solution.py:27
  (15 shorter events, 0.3 us)
Async XLA Ops:
  7.2 112.4 %all-gather.2.cloned.1.call-start = ((), (), s32[]{:S(2)}) async-start(), calls=%async_computation | async-start | bytes 12582912 | tf_op jit(solution)/shard_map/all_gather | solution.py:37
  12.7 205.6 %all-reduce.3.cloned.1.call-start = ((), (), s32[]{:S(2)}) async-start(), calls=%async_computation.1 | async-start | bytes 524288 | tf_op jit(solution)/shard_map/psum | solution.py:38
Sparse Core Ops, SparseCore 0:
  12.8 106.6 all-gather.1
  128.5 89.6 all-reduce.2
where the time goes:
time: 295 us
  waiting for transfers between devices  197 us (67%)
  other arithmetic  59.6 us (20%)
  matrix products  16.8 us (6%)
  between operations  16 us (5%)
  local copies, waits for them, and re-layouts  5.71 us (2%)
    all_gather x1, waiting for transfers between devices, shards(): whole = lax.all_gather(live, 'snap', axis=0, tiled=True)  107 us
    psum x1, waiting for transfers between devices, shards(): gram = lax.psum(gram_of(whole), 'row')  89.8 us
    another operation x6, other arithmetic, factors(): lower = jnp.linalg.cholesky(gram)  34.1 us
    another operation x2, other arithmetic, factors(): lax.linalg.triangular_solve(lower, jnp.eye(width, dtype=jnp.float32), lef...  19.7 us
    dot_general x1, matrix products, gram_of(): lax.dot_general(block, block, (((1,), (1,)), ((), ())), preferred_element...  8.83 us
    dot_general x1, matrix products, apply_weights(): lax.dot_general(weights, block, (((0,), (0,)), ((), ())), preferred_eleme...  6.7 us
  transfers between devices with their start and end apart: 2, of which 2 were waited for; matrix products, arithmetic and copies ran while one was open for 0% of the time, Pallas kernels for 0%

commit v1 on v0

--- a/solution.py
+++ b/solution.py
@@ -1,9 +1,17 @@
+import functools
 import math
 
 import jax
 import jax.numpy as jnp
 from jax import lax
+from jax.experimental import pallas as pl
+from jax.experimental.pallas import tpu as pltpu
 from jax.sharding import PartitionSpec as P
+
+MESH = pl.DeviceIdType.MESH
+HIGH = lax.Precision.HIGHEST
+LANES = 128
+SUBLANES = 8
 
 
 def gram_of(block):
@@ -43,8 +51,365 @@
     return (basis, r_factor)
 
 
+def mxu_nt(a, b):
+    return lax.dot_general(
+        a, b, (((1,), (1,)), ((), ())), preferred_element_type=jnp.float32
+    )
+
+
+def partial_kernel(
+    pieces, counts_ref, x_ref, part_ref, first_ref, later_ref,
+    own, got, mine, theirs,
+    load_sem, send_sem, recv_sem, keep_sem, back_sem, sum_send, sum_recv,
+):
+    snap = lax.axis_index("snap")
+    other = {"snap": 1 - snap}
+    narrow, slots = x_ref.shape
+    half = slots // 2
+    step = half // pieces
+    count = counts_ref[0]
+
+    barrier = pltpu.get_barrier_semaphore()
+    pl.semaphore_signal(barrier, inc=1, device_id=other, device_id_type=MESH)
+
+    loads = []
+    for c in range(2 * pieces):
+        at = pl.ds(c * step, step)
+        copy = pltpu.make_async_copy(x_ref.at[:, at], own.at[:, at], load_sem.at[c])
+        copy.start()
+        loads.append(copy)
+
+    pl.semaphore_wait(barrier, 1)
+    sends = []
+    for c in range(pieces):
+        src = pl.ds(pl.multiple_of(snap * half + c * step, step), step)
+        copy = pltpu.make_async_remote_copy(
+            src_ref=x_ref.at[:, src],
+            dst_ref=got.at[:, pl.ds(c * step, step)],
+            send_sem=send_sem.at[c],
+            recv_sem=recv_sem.at[c],
+            device_id=other,
+            device_id_type=MESH,
+        )
+        copy.start()
+        sends.append(copy)
+
+    def masked(block, start):
+        lane = lax.broadcasted_iota(jnp.int32, block.shape, 1) + start
+        return jnp.where(lane < count, block, jnp.zeros_like(block))
+
+    total = jnp.zeros((narrow, narrow), jnp.float32)
+    for c in range(2 * pieces):
+        loads[c].wait()
+        block = own[:, c * step:(c + 1) * step]
+        total = total + mxu_nt(masked(block, c * step), block)
+    mine[0] = total
+    keep = pltpu.make_async_copy(own.at[:, pl.ds(half, half)], later_ref, keep_sem)
+    keep.start()
+
+    def sum_copy(i):
+        return pltpu.make_async_remote_copy(
+            src_ref=mine.at[i],
+            dst_ref=theirs.at[i],
+            send_sem=sum_send.at[i],
+            recv_sem=sum_recv.at[i],
+            device_id=other,
+            device_id_type=MESH,
+        )
+
+    diagonal = sum_copy(0)
+    diagonal.start()
+
+    cross = jnp.zeros((narrow, narrow), jnp.float32)
+    backs = []
+    base = (1 - snap) * half
+    for c in range(pieces):
+        sends[c].wait_recv()
+        here = pl.ds(c * step, step)
+        back = pltpu.make_async_copy(got.at[:, here], first_ref.at[:, here], back_sem.at[c])
+        back.start()
+        backs.append(back)
+        start = pl.multiple_of(base + c * step, step)
+        block = masked(own[:, pl.ds(start, step)], start)
+        cross = cross + mxu_nt(block, got[:, c * step:(c + 1) * step])
+    mine[1] = jnp.where(snap == 0, cross, cross.T)
+    crossed = sum_copy(1)
+    crossed.start()
+    for copy in sends:
+        copy.wait_send()
+    for copy in backs:
+        copy.wait()
+    keep.wait()
+    diagonal.wait()
+    low = jnp.where(snap == 0, mine[0], theirs[0])
+    high = jnp.where(snap == 0, theirs[0], mine[0])
+    part_ref[0:narrow, :] = low
+    part_ref[narrow:2 * narrow, :] = high
+    crossed.wait()
+    part_ref[2 * narrow:3 * narrow, :] = mine[1] + theirs[1]
+
+
+def partial_grams(snapshots, counts, pieces=8):
+    narrow, slots = snapshots.shape
+    half = slots // 2
+    any_space = pl.BlockSpec(memory_space=pl.ANY)
+    return pl.pallas_call(
+        functools.partial(partial_kernel, pieces),
+        name="partial_grams",
+        out_shape=(
+            jax.ShapeDtypeStruct((3 * narrow, narrow), jnp.float32),
+            jax.ShapeDtypeStruct((narrow, half), snapshots.dtype),
+            jax.ShapeDtypeStruct((narrow, half), snapshots.dtype),
+        ),
+        in_specs=[pl.BlockSpec(memory_space=pltpu.SMEM), any_space],
+        out_specs=(pl.BlockSpec(memory_space=pltpu.VMEM), any_space, any_space),
+        scratch_shapes=[
+            pltpu.VMEM((narrow, slots), snapshots.dtype),
+            pltpu.VMEM((narrow, half), snapshots.dtype),
+            pltpu.VMEM((2, narrow, narrow), jnp.float32),
+            pltpu.VMEM((2, narrow, narrow), jnp.float32),
+            pltpu.SemaphoreType.DMA((2 * pieces,)),
+            pltpu.SemaphoreType.DMA((pieces,)),
+            pltpu.SemaphoreType.DMA((pieces,)),
+            pltpu.SemaphoreType.DMA,
+            pltpu.SemaphoreType.DMA((pieces,)),
+            pltpu.SemaphoreType.DMA((2,)),
+            pltpu.SemaphoreType.DMA((2,)),
+        ],
+        compiler_params=pltpu.CompilerParams(
+            collective_id=0, has_side_effects=True, vmem_limit_bytes=24 << 20
+        ),
+    )(counts, snapshots)
+
+
+def reduce_kernel(n, part_ref, out_ref, parts, send_sem, recv_sem, out_send, out_recv):
+    me = lax.axis_index("row")
+    rows = part_ref.shape[0] // n
+    barrier = pltpu.get_barrier_semaphore()
+    for d in range(1, n):
+        peer = lax.rem(me + d, n)
+        pl.semaphore_signal(barrier, inc=1, device_id={"row": peer}, device_id_type=MESH)
+    pl.semaphore_wait(barrier, n - 1)
+
+    def at(i):
+        return pl.ds(pl.multiple_of(i * rows, SUBLANES), rows)
+
+    copies = []
+    for d in range(1, n):
+        peer = lax.rem(me + d, n)
+        copy = pltpu.make_async_remote_copy(
+            src_ref=part_ref.at[at(peer)],
+            dst_ref=parts.at[d - 1],
+            send_sem=send_sem.at[d - 1],
+            recv_sem=recv_sem.at[d - 1],
+            device_id={"row": peer},
+            device_id_type=MESH,
+        )
+        copy.start()
+        copies.append(copy)
+    total = part_ref[at(me), :]
+    for d in range(1, n):
+        copies[d - 1].wait_recv()
+        total = total + parts[d - 1]
+    out_ref[at(me), :] = total
+    results = []
+    for d in range(1, n):
+        peer = lax.rem(me + d, n)
+        copy = pltpu.make_async_remote_copy(
+            src_ref=out_ref.at[at(me)],
+            dst_ref=out_ref.at[at(me)],
+            send_sem=out_send.at[d - 1],
+            recv_sem=out_recv.at[d - 1],
+            device_id={"row": peer},
+            device_id_type=MESH,
+        )
+        copy.start()
+        results.append(copy)
+    for copy in copies:
+        copy.wait_send()
+    for copy in results:
+        copy.wait()
+
+
+def reduce_rows(part):
+    n = lax.axis_size("row")
+    rows = part.shape[0] // n
+    vmem = pl.BlockSpec(memory_space=pltpu.VMEM)
+    return pl.pallas_call(
+        functools.partial(reduce_kernel, n),
+        name="reduce_rows",
+        out_shape=jax.ShapeDtypeStruct(part.shape, part.dtype),
+        in_specs=[vmem],
+        out_specs=vmem,
+        scratch_shapes=[
+            pltpu.VMEM((n - 1, rows, part.shape[1]), part.dtype),
+            pltpu.SemaphoreType.DMA((n - 1,)),
+            pltpu.SemaphoreType.DMA((n - 1,)),
+            pltpu.SemaphoreType.DMA((n - 1,)),
+            pltpu.SemaphoreType.DMA((n - 1,)),
+        ],
+        compiler_params=pltpu.CompilerParams(
+            collective_id=1, has_side_effects=True, vmem_limit_bytes=8 << 20
+        ),
+        cost_estimate=pl.CostEstimate(
+            flops=1 << 30, bytes_accessed=48 << 20, transcendentals=0
+        ),
+    )(part)
+
+
+def eliminate(groups):
+    shape = groups[0].shape
+    width = shape[1]
+    lane = lax.broadcasted_iota(jnp.int32, shape, 1)
+    sub = lax.broadcasted_iota(jnp.int32, shape, 0)
+    groups = list(groups)
+    for j in range(width):
+        g, p = divmod(j, shape[0])
+        here = lane == j
+        columns = [
+            jnp.broadcast_to(groups[v][:, j:j + 1], shape) for v in range(g, len(groups))
+        ]
+        pivot = jnp.broadcast_to(columns[0][p:p + 1, :], shape)
+        root = lax.rsqrt(pivot)
+        root = root * (1.5 - 0.5 * pivot * root * root)
+        row = jnp.broadcast_to(groups[g][p:p + 1, :], shape)
+        row = jnp.where(here, root, row * root)
+        for v in range(g, len(groups)):
+            left = jnp.where(here, 0.0, groups[v]) - (columns[v - g] * root) * row
+            if v == g:
+                left = jnp.where(sub == p, row, jnp.where(sub > p, left, groups[v]))
+            groups[v] = left
+    return groups
+
+
+def factor_kernel(scale, gram_ref, r_ref, own_ref, other_ref, work, roots):
+    narrow = gram_ref.shape[1]
+    snap = lax.axis_index("snap")
+    row = lax.broadcasted_iota(jnp.int32, (narrow, narrow), 0)
+    col = lax.broadcasted_iota(jnp.int32, (narrow, narrow), 1)
+
+    def dot(a, b, dims):
+        return lax.dot_general(
+            a, b, (dims, ((), ())), precision=HIGH, preferred_element_type=jnp.float32
+        )
+
+    def diagonal(which):
+        full = work[which]
+        inverse = jnp.where(col <= row, full, 0.0)
+        upper = jnp.where(col > row, full, 0.0)
+        upper = jnp.where(col == row, 1.0 / full, upper)
+        return inverse, upper
+
+    work[0] = gram_ref[0:narrow, :]
+    work[1] = gram_ref[narrow:2 * narrow, :]
+
+    @pl.loop(0, 2)
+    def _(block):
+        groups = [
+            work[block, SUBLANES * v:SUBLANES * (v + 1), :] for v in range(narrow // SUBLANES)
+        ]
+        for v, group in enumerate(eliminate(groups)):
+            work[block, SUBLANES * v:SUBLANES * (v + 1), :] = group
+
+        @pl.when(block == 0)
+        def _():
+            inverse, _ = diagonal(0)
+            right = dot(inverse, gram_ref[2 * narrow:3 * narrow, :], ((1,), (0,)))
+            roots[...] = right
+            work[1] = work[1] - dot(right, right, ((0,), (0,)))
+
+    inverse0, upper0 = diagonal(0)
+    inverse1, upper1 = diagonal(1)
+    right = roots[...]
+    below = -dot(inverse1, dot(right, inverse0, ((0,), (0,))), ((1,), (0,)))
+    r_ref[0:narrow, 0:narrow] = upper0 / scale
+    r_ref[0:narrow, narrow:] = right / scale
+    r_ref[narrow:, 0:narrow] = jnp.zeros_like(right)
+    r_ref[narrow:, narrow:] = upper1 / scale
+    own = jnp.where(snap == 0, inverse0, inverse1)
+    own_ref[...] = (own * scale).astype(own_ref.dtype)
+    other = jnp.where(snap == 0, 0.0, below)
+    other_ref[...] = (other * scale).astype(other_ref.dtype)
+
+
+def factor(gram, scale, dtype):
+    narrow = gram.shape[1]
+    vmem = pl.BlockSpec(memory_space=pltpu.VMEM)
+    return pl.pallas_call(
+        functools.partial(factor_kernel, scale),
+        name="factor",
+        out_shape=(
+            jax.ShapeDtypeStruct((2 * narrow, 2 * narrow), jnp.float32),
+            jax.ShapeDtypeStruct((narrow, narrow), dtype),
+            jax.ShapeDtypeStruct((narrow, narrow), dtype),
+        ),
+        in_specs=[vmem],
+        out_specs=(vmem, vmem, vmem),
+        scratch_shapes=[
+            pltpu.VMEM((2, narrow, narrow), jnp.float32),
+            pltpu.VMEM((narrow, narrow), jnp.float32),
+        ],
+        compiler_params=pltpu.CompilerParams(vmem_limit_bytes=8 << 20),
+        cost_estimate=pl.CostEstimate(
+            flops=1 << 30, bytes_accessed=96 << 20, transcendentals=0
+        ),
+    )(gram)
+
+
+def basis_kernel(parts, counts_ref, own_w, other_w, own_ref, first_ref, later_ref, out_ref):
+    c = pl.program_id(0)
+    width = out_ref.shape[1]
+    got = jnp.where(c < parts // 2, first_ref[...], later_ref[...])
+    value = lax.dot_general(
+        own_w[...], own_ref[...], (((1,), (0,)), ((), ())), preferred_element_type=jnp.float32
+    ) + lax.dot_general(
+        other_w[...], got, (((1,), (0,)), ((), ())), preferred_element_type=jnp.float32
+    )
+    lane = lax.broadcasted_iota(jnp.int32, out_ref.shape, 1) + c * width
+    out_ref[...] = jnp.where(lane < counts_ref[0], value, 0.0).astype(out_ref.dtype)
+
+
+def form_basis(counts, own_w, other_w, snapshots, first, later, parts=8):
+    narrow, slots = snapshots.shape
+    width = slots // parts
+    mid = parts // 2
+    small = pl.BlockSpec((narrow, narrow), lambda c: (0, 0))
+    return pl.pallas_call(
+        functools.partial(basis_kernel, parts),
+        name="form_basis",
+        grid=(parts,),
+        out_shape=jax.ShapeDtypeStruct(snapshots.shape, snapshots.dtype),
+        in_specs=[
+            pl.BlockSpec(memory_space=pltpu.SMEM),
+            small,
+            small,
+            pl.BlockSpec((narrow, width), lambda c: (0, c)),
+            pl.BlockSpec((narrow, width), lambda c: (0, jnp.minimum(c, mid - 1))),
+            pl.BlockSpec((narrow, width), lambda c: (0, jnp.maximum(c - mid, 0))),
+        ],
+        out_specs=pl.BlockSpec((narrow, width), lambda c: (0, c)),
+        compiler_params=pltpu.CompilerParams(vmem_limit_bytes=16 << 20),
+    )(counts, own_w, other_w, snapshots, first, later)
+
+
+def halves(snapshots, counts):
+    slots = snapshots.shape[1]
+    scale = math.sqrt(slots * lax.axis_size("row"))
+    part, first, later = partial_grams(snapshots, counts)
+    later = lax.ppermute(later, "snap", [(0, 1)])
+    gram = reduce_rows(part)
+    r_factor, own_w, other_w = factor(gram, scale, snapshots.dtype)
+    basis = form_basis(counts, own_w, other_w, snapshots, first, later)
+    return (basis, r_factor)
+
+
+def two_halves(mesh):
+    return mesh.shape["snap"] == 2 and mesh.shape["row"] == 16
+
+
 def solution(mesh):
     placed = (P("snap", "row"), P("row"))
+    body = halves if two_halves(mesh) else shards
     return jax.shard_map(
-        shards, mesh=mesh, in_specs=placed, out_specs=(P("snap", "row"), P()), check_vma=False
+        body, mesh=mesh, in_specs=placed, out_specs=(P("snap", "row"), P()), check_vma=False
     )

time: 295 us -> 120 us (0.41)
  waiting for transfers between devices: 197 us -> 0.01 us
  Pallas kernels: 0 us -> 113 us
  other arithmetic: 59.6 us -> 0 us
  matrix products: 16.8 us -> 0 us
  between operations: 16 us -> 1.32 us
  local copies, waits for them, and re-layouts: 5.71 us -> 2.19 us
    pallas_call x0 -> x4, Pallas kernels: none -> 113 us  [the longest x1 54.1 us: partial_grams(): pl.pallas_call(functools.partial(partial_kernel, pieces), name='partial_g...]
    all_gather x1 -> x0, waiting for transfers between devices: 107 us -> none  [shards(): whole = lax.all_gather(live, 'snap', axis=0, tiled=True)]
    psum x1 -> x0, waiting for transfers between devices: 89.8 us -> none  [shards(): gram = lax.psum(gram_of(whole), 'row')]
    another operation x8 -> x0, other arithmetic: 53.7 us -> none  [the longest x6 34.1 us: factors(): lower = jnp.linalg.cholesky(gram)]
    dot_general x2 -> x0, matrix products: 15.5 us -> none  [the longest x1 8.83 us: gram_of(): lax.dot_general(block, block, (((1,), (1,)), ((), ())), preferred_element...]
    select_n x1 -> x0, other arithmetic: 4.78 us -> none  [shards(): live = jnp.where(slot < counts[0], snapshots, jnp.zeros_like(snapshots))]
    another operation x9 -> x0, local copies, waits for them, and re-layouts: 3.79 us -> none
  transfers between devices with their start and end apart: 2 -> 1, of which waited for: 2 -> 0; matrix products, arithmetic and copies ran while one was open for 0% -> 0% of each run, Pallas kernels for 0% -> 45%
where the time goes in v1:
time: 120 us
  Pallas kernels  113 us (94%)
  starting transfers between devices  2.62 us (2%)
  local copies, waits for them, and re-layouts  2.19 us (2%)
  between operations  1.32 us (1%)
    pallas_call x1, Pallas kernels, partial_grams(): pl.pallas_call(functools.partial(partial_kernel, pieces), name='partial_g...  54.1 us
    pallas_call x1, Pallas kernels, factor(): pl.pallas_call(functools.partial(factor_kernel, scale), name='factor', ou...  37.6 us
    pallas_call x1, Pallas kernels, reduce_rows(): pl.pallas_call(functools.partial(reduce_kernel, n), name='reduce_rows', o...  16 us
    pallas_call x1, Pallas kernels, form_basis(): pl.pallas_call(functools.partial(basis_kernel, parts), name='form_basis',...  5.75 us
    ppermute x1, starting transfers between devices, halves(): later = lax.ppermute(later, 'snap', [(0, 1)])  2.62 us
  transfers between devices with their start and end apart: 1, of which 0 were waited for; matrix products, arithmetic and copies ran while one was open for 0% of the time, Pallas kernels for 45%

profile of v1, /device:TPU:0, one launch (start us, length us, event | category | flops | bytes accessed | tf_op | source)
XLA Modules:
  0.0 119.6 jit_solution(11540340511671878124)
XLA Ops:
  1.3 0.0 copy-start
  1.3 2.2 %copy-done = bf16[128,16384]{1,0:T(8,128)(2,1)S(1)} copy-done((bf16[128,16384]{1,0:T(8,128)(2,1)S(1)}, bf16[128,16384]{1,0:T(8,128)(2,1)}, u32[]{:S(2)}) %copy-start) | copy-done | bytes 4194328
  3.5 54.1 %partial_grams.1 = (f32[384,128]{1,0:T(8,128)S(1)}, bf16[128,8192]{1,0:T(8,128)(2,1)S(1)}, bf16[128,8192]{1,0:T(8,128)(2,1)S(1)}) custom-call(s32[1]{0:T(128)S(6)} %copy.4.counts_ref, bf16[128,16384]{1,0:T(8,128)(2,1)S(1)} %copy-done), custom_call_target="tpu_custom_call" | custom-call | tf_op jit(solution)/shard_map/partial_grams/pallas_call | solution.py:156
  57.5 2.6 %collective-permute-start = (bf16[128,8192]{1,0:T(8,128)(2,1)S(1)}, bf16[128,8192]{1,0:T(8,128)(2,1)S(1)}, u32[]{:S(2)}, u32[]{:S(2)}) collective-permute-start(bf16[128,8192]{1,0:T(8,128)(2,1)S(1)} %get-tuple-element.12), channel_id=1, source_target_pairs={{0,16},{1,17},{2,18},{3,19},{4,20},{5,21},{6,22},{7,23},{8,24},{9,... | collective-permute-start | bytes 6291464 | tf_op jit(solution)/shard_map/ppermute | solution.py:399
  60.2 0.0 copy-start.1
  60.2 16.0 %reduce_rows.1.gram_ref = f32[384,128]{1,0:T(8,128)S(1)} custom-call(f32[384,128]{1,0:T(8,128)S(1)} %get-tuple-element.8.part_ref), custom_call_target="tpu_custom_call" | custom-call | flops 1073741824 | bytes 50331648 | tf_op jit(solution)/shard_map/reduce_rows/pallas_call | solution.py:238
  76.2 37.6 %factor.1 = (f32[256,256]{1,0:T(8,128)}, bf16[128,128]{1,0:T(8,128)(2,1)S(1)}, bf16[128,128]{1,0:T(8,128)(2,1)S(1)}) custom-call(f32[384,128]{1,0:T(8,128)S(1)} %reduce_rows.1.gram_ref), custom_call_target="tpu_custom_call" | custom-call | flops 1073741824 | bytes 100663296 | tf_op jit(solution)/shard_map/factor/pallas_call | solution.py:338
  113.8 0.0 collective-permute-done.later_ref
  113.8 0.0 copy-done.1
  113.8 5.8 %form_basis.1 = bf16[128,16384]{1,0:T(8,128)(2,1)} custom-call(s32[1]{0:T(128)S(6)} %copy.4.counts_ref, bf16[128,128]{1,0:T(8,128)(2,1)S(1)} %get-tuple-element.9.own_w, bf16[128,128]{1,0:T(8,128)(2,1)S(1)} %get-tuple-element.10.other_w, bf16[128,16384]{1,0:T(8,128)(2,1)S(1)} %copy-done.1, bf16[128,8192]{1,0:T(8,128)(2,1)S(1)} %get-tuple-element.11.first_ref, ...), custom_call_target="tpu_custom_call" | custom-call | tf_op jit(solution)/shard_map/form_basis/pallas_call | solution.py:377
Async XLA Ops:
  1.3 2.2 %copy-start = (bf16[128,16384]{1,0:T(8,128)(2,1)S(1)}, bf16[128,16384]{1,0:T(8,128)(2,1)}, u32[]{:S(2)}) copy-start(bf16[128,16384]{1,0:T(8,128)(2,1)} %own_ref.1) | copy-start | bytes 12582916
  57.5 56.3 %collective-permute-start = (bf16[128,8192]{1,0:T(8,128)(2,1)S(1)}, bf16[128,8192]{1,0:T(8,128)(2,1)S(1)}, u32[]{:S(2)}, u32[]{:S(2)}) collective-permute-start(bf16[128,8192]{1,0:T(8,128)(2,1)S(1)} %get-tuple-element.12), channel_id=1, source_target_pairs={{0,16},{1,17},{2,18},{3,19},{4,20},{5,21},{6,22},{7,23},{8,24},{9,... | collective-permute-start | bytes 6291464 | tf_op jit(solution)/shard_map/ppermute | solution.py:399
  60.2 53.7 %copy-start.1 = (bf16[128,16384]{1,0:T(8,128)(2,1)S(1)}, bf16[128,16384]{1,0:T(8,128)(2,1)}, u32[]{:S(2)}) copy-start(bf16[128,16384]{1,0:T(8,128)(2,1)} %own_ref.1) | copy-start | bytes 12582916

commit v2 on v1

--- a/solution.py
+++ b/solution.py
@@ -161,7 +161,10 @@
             jax.ShapeDtypeStruct((narrow, half), snapshots.dtype),
             jax.ShapeDtypeStruct((narrow, half), snapshots.dtype),
         ),
-        in_specs=[pl.BlockSpec(memory_space=pltpu.SMEM), any_space],
+        in_specs=[
+            pl.BlockSpec(memory_space=pltpu.SMEM),
+            pl.BlockSpec(memory_space=pltpu.HBM),
+        ],
         out_specs=(pl.BlockSpec(memory_space=pltpu.VMEM), any_space, any_space),
         scratch_shapes=[
             pltpu.VMEM((narrow, slots), snapshots.dtype),
@@ -177,7 +180,7 @@
             pltpu.SemaphoreType.DMA((2,)),
         ],
         compiler_params=pltpu.CompilerParams(
-            collective_id=0, has_side_effects=True, vmem_limit_bytes=24 << 20
+            collective_id=0, has_side_effects=True, vmem_limit_bytes=62 << 20
         ),
     )(counts, snapshots)
 
@@ -259,26 +262,40 @@
 
 def eliminate(groups):
     shape = groups[0].shape
-    width = shape[1]
+    tall = shape[0]
     lane = lax.broadcasted_iota(jnp.int32, shape, 1)
     sub = lax.broadcasted_iota(jnp.int32, shape, 0)
     groups = list(groups)
-    for j in range(width):
-        g, p = divmod(j, shape[0])
-        here = lane == j
+    count = len(groups)
+
+    def line(block, p):
+        return jnp.broadcast_to(block[p:p + 1, :], shape)
+
+    for g in range(count):
         columns = [
-            jnp.broadcast_to(groups[v][:, j:j + 1], shape) for v in range(g, len(groups))
+            [
+                jnp.broadcast_to(groups[v][:, g * tall + q:g * tall + q + 1], shape)
+                for v in range(g, count)
+            ]
+            for q in range(tall)
         ]
-        pivot = jnp.broadcast_to(columns[0][p:p + 1, :], shape)
-        root = lax.rsqrt(pivot)
-        root = root * (1.5 - 0.5 * pivot * root * root)
-        row = jnp.broadcast_to(groups[g][p:p + 1, :], shape)
-        row = jnp.where(here, root, row * root)
-        for v in range(g, len(groups)):
-            left = jnp.where(here, 0.0, groups[v]) - (columns[v - g] * root) * row
-            if v == g:
-                left = jnp.where(sub == p, row, jnp.where(sub > p, left, groups[v]))
-            groups[v] = left
+        for p in range(tall):
+            here = lane == g * tall + p
+            pivot = line(columns[p][0], p)
+            root = lax.rsqrt(pivot)
+            root = root * (1.5 - 0.5 * pivot * root * root)
+            lefts = [column * root for column in columns[p]]
+            lefts[0] = jnp.where(sub > p, lefts[0], 0.0)
+            for q in range(p + 1, tall):
+                top = line(columns[q][0], p) * root
+                columns[q] = [c - m * top for c, m in zip(columns[q], lefts)]
+            row = jnp.where(here, root, line(groups[g], p) * root)
+            for v in range(g, count):
+                old = groups[v]
+                new = jnp.where(here, 0.0, old) - lefts[v - g] * row
+                if v == g:
+                    new = jnp.where(sub == p, row, jnp.where(sub > p, new, old))
+                groups[v] = new
     return groups
 
 
@@ -356,40 +373,64 @@
     )(gram)
 
 
-def basis_kernel(parts, counts_ref, own_w, other_w, own_ref, first_ref, later_ref, out_ref):
-    c = pl.program_id(0)
-    width = out_ref.shape[1]
-    got = jnp.where(c < parts // 2, first_ref[...], later_ref[...])
-    value = lax.dot_general(
-        own_w[...], own_ref[...], (((1,), (0,)), ((), ())), preferred_element_type=jnp.float32
-    ) + lax.dot_general(
-        other_w[...], got, (((1,), (0,)), ((), ())), preferred_element_type=jnp.float32
-    )
-    lane = lax.broadcasted_iota(jnp.int32, out_ref.shape, 1) + c * width
-    out_ref[...] = jnp.where(lane < counts_ref[0], value, 0.0).astype(out_ref.dtype)
-
-
-def form_basis(counts, own_w, other_w, snapshots, first, later, parts=8):
-    narrow, slots = snapshots.shape
-    width = slots // parts
-    mid = parts // 2
-    small = pl.BlockSpec((narrow, narrow), lambda c: (0, 0))
+def basis_kernel(
+    pieces, first_piece, counts_ref, own_w, other_w, own_ref, got_ref, *rest
+):
+    out_ref, stage, sems = rest[-3:]
+    narrow, width = got_ref.shape
+    step = width // pieces
+    count = counts_ref[0]
+    weights = jnp.concatenate([own_w[...], other_w[...]], axis=1)
+    copies = []
+    for c in range(pieces):
+        here = pl.ds(c * step, step)
+        start = first_piece + c * step
+        both = jnp.concatenate(
+            [own_ref[:, start:start + step], got_ref[:, c * step:(c + 1) * step]], axis=0
+        )
+        value = lax.dot_general(
+            weights, both, (((1,), (0,)), ((), ())), preferred_element_type=jnp.float32
+        )
+        lane = lax.broadcasted_iota(jnp.int32, value.shape, 1) + start
+        stage[:, c * step:(c + 1) * step] = jnp.where(lane < count, value, 0.0).astype(stage.dtype)
+        copy = pltpu.make_async_copy(
+            stage.at[:, here], out_ref.at[:, pl.ds(start, step)], sems.at[c]
+        )
+        copy.start()
+        copies.append(copy)
+    for copy in copies:
+        copy.wait()
+
+
+def form_basis(counts, own_w, other_w, snapshots, got, start, before=None, pieces=4):
+    narrow, width = got.shape
+    vmem = pl.BlockSpec(memory_space=pltpu.VMEM)
+    hbm = pl.BlockSpec(memory_space=pltpu.HBM)
+    operands = [counts, own_w, other_w, snapshots, got]
+    specs = [pl.BlockSpec(memory_space=pltpu.SMEM), vmem, vmem, vmem, vmem]
+    aliases = {}
+    if before is not None:
+        aliases = {len(operands): 0}
+        operands.append(before)
+        specs.append(hbm)
     return pl.pallas_call(
-        functools.partial(basis_kernel, parts),
+        functools.partial(basis_kernel, pieces, start),
         name="form_basis",
-        grid=(parts,),
         out_shape=jax.ShapeDtypeStruct(snapshots.shape, snapshots.dtype),
-        in_specs=[
-            pl.BlockSpec(memory_space=pltpu.SMEM),
-            small,
-            small,
-            pl.BlockSpec((narrow, width), lambda c: (0, c)),
-            pl.BlockSpec((narrow, width), lambda c: (0, jnp.minimum(c, mid - 1))),
-            pl.BlockSpec((narrow, width), lambda c: (0, jnp.maximum(c - mid, 0))),
+        in_specs=specs,
+        out_specs=hbm,
+        input_output_aliases=aliases,
+        scratch_shapes=[
+            pltpu.VMEM((narrow, width), snapshots.dtype),
+            pltpu.SemaphoreType.DMA((pieces,)),
         ],
-        out_specs=pl.BlockSpec((narrow, width), lambda c: (0, c)),
         compiler_params=pltpu.CompilerParams(vmem_limit_bytes=16 << 20),
-    )(counts, own_w, other_w, snapshots, first, later)
+        cost_estimate=pl.CostEstimate(
+            flops=4 * narrow * narrow * width,
+            bytes_accessed=8 * narrow * width,
+            transcendentals=0,
+        ),
+    )(*operands)
 
 
 def halves(snapshots, counts):
@@ -399,7 +440,9 @@
     later = lax.ppermute(later, "snap", [(0, 1)])
     gram = reduce_rows(part)
     r_factor, own_w, other_w = factor(gram, scale, snapshots.dtype)
-    basis = form_basis(counts, own_w, other_w, snapshots, first, later)
+    half = snapshots.shape[1] // 2
+    basis = form_basis(counts, own_w, other_w, snapshots, first, 0)
+    basis = form_basis(counts, own_w, other_w, snapshots, later, half, basis)
     return (basis, r_factor)
 
 

time: 120 us -> 104 us (0.87)
  Pallas kernels: 113 us -> 87 us
  waiting for transfers between devices: 0.01 us -> 12.4 us
  local copies, waits for them, and re-layouts: 2.19 us -> 0.93 us
    pallas_call x1, Pallas kernels: 37.6 us -> 12.6 us  [factor(): pl.pallas_call(functools.partial(factor_kernel, scale), name='factor', ou...]
    ppermute x1, waiting for transfers between devices: 0.01 us -> 12.4 us  [halves(): later = lax.ppermute(later, 'snap', [(0, 1)])]
    pallas_call x1 -> x2, Pallas kernels: 5.75 us -> 3.32 us  [form_basis(): pl.pallas_call(functools.partial(basis_kernel, pieces, start), name='form...]
    unnamed x4 -> x6, local copies, waits for them, and re-layouts: 2.19 us -> 0.93 us
  transfers between devices with their start and end apart: 1 -> 1, of which waited for: 0 -> 1; matrix products, arithmetic and copies ran while one was open for 0% -> 0% of each run, Pallas kernels for 45% -> 29%
where the time goes in v2:
time: 104 us
  Pallas kernels  87 us (84%)
  waiting for transfers between devices  12.4 us (12%)
  starting transfers between devices  2.63 us (3%)
  between operations  1.33 us (1%)
    pallas_call x1, Pallas kernels, partial_grams(): pl.pallas_call(functools.partial(partial_kernel, pieces), name='partial_g...  55 us
    pallas_call x1, Pallas kernels, reduce_rows(): pl.pallas_call(functools.partial(reduce_kernel, n), name='reduce_rows', o...  16.1 us
    pallas_call x1, Pallas kernels, factor(): pl.pallas_call(functools.partial(factor_kernel, scale), name='factor', ou...  12.6 us
    ppermute x1, waiting for transfers between devices, halves(): later = lax.ppermute(later, 'snap', [(0, 1)])  12.4 us
    pallas_call x2, Pallas kernels, form_basis(): pl.pallas_call(functools.partial(basis_kernel, pieces, start), name='form...  3.32 us
    ppermute x1, starting transfers between devices, halves(): later = lax.ppermute(later, 'snap', [(0, 1)])  2.63 us
  transfers between devices with their start and end apart: 1, of which 1 were waited for; matrix products, arithmetic and copies ran while one was open for 0% of the time, Pallas kernels for 29%

profile of v2, /device:TPU:0, one launch (start us, length us, event | category | flops | bytes accessed | tf_op | source)
XLA Modules:
  0.0 104.3 jit_solution(5813217847280572587)
XLA Ops:
  1.3 55.0 %partial_grams.1 = (f32[384,128]{1,0:T(8,128)}, bf16[128,8192]{1,0:T(8,128)(2,1)}, bf16[128,8192]{1,0:T(8,128)(2,1)}) custom-call(s32[1]{0:T(128)S(6)} %copy.6.counts_ref, bf16[128,16384]{1,0:T(8,128)(2,1)} %own_ref.3), custom_call_target="tpu_custom_call" | custom-call | tf_op jit(solution)/shard_map/partial_grams/pallas_call | solution.py:156
  56.2 0.0 copy-start
  56.2 0.0 copy-start.1
  56.3 2.6 %collective-permute-start = (bf16[128,8192]{1,0:T(8,128)(2,1)}, bf16[128,8192]{1,0:T(8,128)(2,1)S(1)}, u32[]{:S(2)}, u32[]{:S(2)}) collective-permute-start(bf16[128,8192]{1,0:T(8,128)(2,1)} %get-tuple-element.11), channel_id=1, source_target_pairs={{0,16},{1,17},{2,18},{3,19},{4,20},{5,21},{6,22},{7,23},{8,24},{9,... | collective-permute-start | bytes 6291464 | tf_op jit(solution)/shard_map/ppermute | solution.py:440
  58.9 0.0 copy-start.2
  58.9 0.9 copy-done.2
  59.8 16.1 %reduce_rows.1.gram_ref = f32[384,128]{1,0:T(8,128)S(1)} custom-call(f32[384,128]{1,0:T(8,128)S(1)} %copy-done.2), custom_call_target="tpu_custom_call" | custom-call | flops 1073741824 | bytes 50331648 | tf_op jit(solution)/shard_map/reduce_rows/pallas_call | solution.py:241
  76.0 12.6 %factor.1 = (f32[256,256]{1,0:T(8,128)}, bf16[128,128]{1,0:T(8,128)(2,1)S(1)}, bf16[128,128]{1,0:T(8,128)(2,1)S(1)}) custom-call(f32[384,128]{1,0:T(8,128)S(1)} %reduce_rows.1.gram_ref), custom_call_target="tpu_custom_call" | custom-call | flops 1073741824 | bytes 100663296 | tf_op jit(solution)/shard_map/factor/pallas_call | solution.py:355
  88.6 0.0 copy-done
  88.6 0.0 copy-done.1
  88.6 1.7 %form_basis.2.rest_0_ = bf16[128,16384]{1,0:T(8,128)(2,1)} custom-call(s32[1]{0:T(128)S(6)} %copy.6.counts_ref, bf16[128,128]{1,0:T(8,128)(2,1)S(1)} %get-tuple-element.9.own_w, bf16[128,128]{1,0:T(8,128)(2,1)S(1)} %get-tuple-element.10.other_w, bf16[128,16384]{1,0:T(8,128)(2,1)S(1)} %copy-done, bf16[128,8192]{1,0:T(8,128)(2,1)S(1)} %copy-done.1), custom_call_target="tpu_custom_call" | custom-call | flops 536870912 | bytes 8388608 | tf_op jit(solution)/shard_map/form_basis/pallas_call | solution.py:416
  90.3 12.4 %collective-permute-done.got_ref = bf16[128,8192]{1,0:T(8,128)(2,1)S(1)} collective-permute-done((bf16[128,8192]{1,0:T(8,128)(2,1)}, bf16[128,8192]{1,0:T(8,128)(2,1)S(1)}, u32[]{:S(2)}, u32[]{:S(2)}) %collective-permute-start) | collective-permute-done | bytes 2097184 | tf_op jit(solution)/shard_map/ppermute | solution.py:440
  102.6 1.7 %form_basis.3 = bf16[128,16384]{1,0:T(8,128)(2,1)} custom-call(s32[1]{0:T(128)S(6)} %copy.6.counts_ref, bf16[128,128]{1,0:T(8,128)(2,1)S(1)} %get-tuple-element.9.own_w, bf16[128,128]{1,0:T(8,128)(2,1)S(1)} %get-tuple-element.10.other_w, bf16[128,16384]{1,0:T(8,128)(2,1)S(1)} %copy-done, ...), custom_call_target="tpu_custom_call", output_to_operand_aliasing={{}: (5, {})} | custom-call | flops 536870912 | bytes 8388608 | tf_op jit(solution)/shard_map/form_basis/pallas_call | solution.py:416
Async XLA Ops:
  56.2 32.3 %copy-start = (bf16[128,16384]{1,0:T(8,128)(2,1)S(1)}, bf16[128,16384]{1,0:T(8,128)(2,1)}, u32[]{:S(2)}) copy-start(bf16[128,16384]{1,0:T(8,128)(2,1)} %own_ref.3) | copy-start | bytes 12582916
  56.2 32.3 %copy-start.1 = (bf16[128,8192]{1,0:T(8,128)(2,1)S(1)}, bf16[128,8192]{1,0:T(8,128)(2,1)}, u32[]{:S(2)}) copy-start(bf16[128,8192]{1,0:T(8,128)(2,1)} %get-tuple-element.12.got_ref) | copy-start | bytes 6291460
  56.3 46.4 %collective-permute-start = (bf16[128,8192]{1,0:T(8,128)(2,1)}, bf16[128,8192]{1,0:T(8,128)(2,1)S(1)}, u32[]{:S(2)}, u32[]{:S(2)}) collective-permute-start(bf16[128,8192]{1,0:T(8,128)(2,1)} %get-tuple-element.11), channel_id=1, source_target_pairs={{0,16},{1,17},{2,18},{3,19},{4,20},{5,21},{6,22},{7,23},{8,24},{9,... | collective-permute-start | bytes 6291464 | tf_op jit(solution)/shard_map/ppermute | solution.py:440
  58.9 0.9 copy-start.2

commit v3 on v2

--- a/solution.py
+++ b/solution.py
@@ -58,7 +58,7 @@
 
 
 def partial_kernel(
-    pieces, counts_ref, x_ref, part_ref, first_ref, later_ref,
+    pieces, counts_ref, x_ref, part_ref, first_ref, later_ref, last_ref,
     own, got, mine, theirs,
     load_sem, send_sem, recv_sem, keep_sem, back_sem, sum_send, sum_recv,
 ):
@@ -80,19 +80,23 @@
         loads.append(copy)
 
     pl.semaphore_wait(barrier, 1)
-    sends = []
-    for c in range(pieces):
-        src = pl.ds(pl.multiple_of(snap * half + c * step, step), step)
+
+    def send(i, src, dst, size):
         copy = pltpu.make_async_remote_copy(
-            src_ref=x_ref.at[:, src],
-            dst_ref=got.at[:, pl.ds(c * step, step)],
-            send_sem=send_sem.at[c],
-            recv_sem=recv_sem.at[c],
+            src_ref=x_ref.at[:, pl.ds(src, size)],
+            dst_ref=got.at[:, pl.ds(dst, size)],
+            send_sem=send_sem.at[i],
+            recv_sem=recv_sem.at[i],
             device_id=other,
             device_id_type=MESH,
         )
         copy.start()
-        sends.append(copy)
+        return copy
+
+    sends = [
+        send(c, pl.multiple_of(snap * half + c * step, step), c * step, step)
+        for c in range(pieces)
+    ]
 
     def masked(block, start):
         lane = lax.broadcasted_iota(jnp.int32, block.shape, 1) + start
@@ -104,8 +108,14 @@
         block = own[:, c * step:(c + 1) * step]
         total = total + mxu_nt(masked(block, c * step), block)
     mine[0] = total
-    keep = pltpu.make_async_copy(own.at[:, pl.ds(half, half)], later_ref, keep_sem)
-    keep.start()
+    keeps = []
+    start = first_ref.shape[1]
+    for i, ref in enumerate((later_ref, last_ref)):
+        size = ref.shape[1]
+        keep = pltpu.make_async_copy(own.at[:, pl.ds(start, size)], ref, keep_sem.at[i])
+        keep.start()
+        keeps.append(keep)
+        start += size
 
     def sum_copy(i):
         return pltpu.make_async_remote_copy(
@@ -119,6 +129,8 @@
 
     diagonal = sum_copy(0)
     diagonal.start()
+    ahead = (first_ref.shape[1] - half) // 2
+    extras = [send(pieces, half, half, ahead)]
 
     cross = jnp.zeros((narrow, narrow), jnp.float32)
     backs = []
@@ -135,11 +147,11 @@
     mine[1] = jnp.where(snap == 0, cross, cross.T)
     crossed = sum_copy(1)
     crossed.start()
+    extras.append(send(pieces + 1, half + ahead, half + ahead, ahead))
     for copy in sends:
         copy.wait_send()
-    for copy in backs:
+    for copy in keeps:
         copy.wait()
-    keep.wait()
     diagonal.wait()
     low = jnp.where(snap == 0, mine[0], theirs[0])
     high = jnp.where(snap == 0, theirs[0], mine[0])
@@ -147,35 +159,50 @@
     part_ref[narrow:2 * narrow, :] = high
     crossed.wait()
     part_ref[2 * narrow:3 * narrow, :] = mine[1] + theirs[1]
+    for i, copy in enumerate(extras):
+        copy.wait()
+        here = pl.ds(half + i * ahead, ahead)
+        back = pltpu.make_async_copy(
+            got.at[:, here], first_ref.at[:, here], back_sem.at[pieces + i]
+        )
+        back.start()
+        backs.append(back)
+    for copy in backs:
+        copy.wait()
 
 
 def partial_grams(snapshots, counts, pieces=8):
     narrow, slots = snapshots.shape
     half = slots // 2
+    step = half // pieces
+    early = half + step
+    last = 2 * step
+    later = slots - early - last
     any_space = pl.BlockSpec(memory_space=pl.ANY)
     return pl.pallas_call(
         functools.partial(partial_kernel, pieces),
         name="partial_grams",
         out_shape=(
             jax.ShapeDtypeStruct((3 * narrow, narrow), jnp.float32),
-            jax.ShapeDtypeStruct((narrow, half), snapshots.dtype),
-            jax.ShapeDtypeStruct((narrow, half), snapshots.dtype),
+            jax.ShapeDtypeStruct((narrow, early), snapshots.dtype),
+            jax.ShapeDtypeStruct((narrow, later), snapshots.dtype),
+            jax.ShapeDtypeStruct((narrow, last), snapshots.dtype),
         ),
         in_specs=[
             pl.BlockSpec(memory_space=pltpu.SMEM),
             pl.BlockSpec(memory_space=pltpu.HBM),
         ],
-        out_specs=(pl.BlockSpec(memory_space=pltpu.VMEM), any_space, any_space),
+        out_specs=(pl.BlockSpec(memory_space=pltpu.VMEM), any_space, any_space, any_space),
         scratch_shapes=[
             pltpu.VMEM((narrow, slots), snapshots.dtype),
-            pltpu.VMEM((narrow, half), snapshots.dtype),
+            pltpu.VMEM((narrow, early), snapshots.dtype),
             pltpu.VMEM((2, narrow, narrow), jnp.float32),
             pltpu.VMEM((2, narrow, narrow), jnp.float32),
             pltpu.SemaphoreType.DMA((2 * pieces,)),
-            pltpu.SemaphoreType.DMA((pieces,)),
-            pltpu.SemaphoreType.DMA((pieces,)),
-            pltpu.SemaphoreType.DMA,
-            pltpu.SemaphoreType.DMA((pieces,)),
+            pltpu.SemaphoreType.DMA((pieces + 2,)),
+            pltpu.SemaphoreType.DMA((pieces + 2,)),
+            pltpu.SemaphoreType.DMA((2,)),
+            pltpu.SemaphoreType.DMA((pieces + 2,)),
             pltpu.SemaphoreType.DMA((2,)),
             pltpu.SemaphoreType.DMA((2,)),
         ],
@@ -402,8 +429,9 @@
         copy.wait()
 
 
-def form_basis(counts, own_w, other_w, snapshots, got, start, before=None, pieces=4):
+def form_basis(counts, own_w, other_w, snapshots, got, start, before=None, most=2048):
     narrow, width = got.shape
+    pieces = next(n for n in range(1, width) if width % (n * LANES) == 0 and width // n <= most)
     vmem = pl.BlockSpec(memory_space=pltpu.VMEM)
     hbm = pl.BlockSpec(memory_space=pltpu.HBM)
     operands = [counts, own_w, other_w, snapshots, got]
@@ -436,13 +464,14 @@
 def halves(snapshots, counts):
     slots = snapshots.shape[1]
     scale = math.sqrt(slots * lax.axis_size("row"))
-    part, first, later = partial_grams(snapshots, counts)
-    later = lax.ppermute(later, "snap", [(0, 1)])
+    part, *got = partial_grams(snapshots, counts)
+    got[1:] = [lax.ppermute(piece, "snap", [(0, 1)]) for piece in got[1:]]
     gram = reduce_rows(part)
     r_factor, own_w, other_w = factor(gram, scale, snapshots.dtype)
-    half = snapshots.shape[1] // 2
-    basis = form_basis(counts, own_w, other_w, snapshots, first, 0)
-    basis = form_basis(counts, own_w, other_w, snapshots, later, half, basis)
+    basis, start = None, 0
+    for piece in got:
+        basis = form_basis(counts, own_w, other_w, snapshots, piece, start, basis)
+        start += piece.shape[1]
     return (basis, r_factor)
 
 

time: 104 us -> 104 us (level)
  waiting for transfers between devices: 12.4 us -> 4.64 us
  Pallas kernels: 87 us -> 91.9 us
  starting transfers between devices: 2.63 us -> 5.32 us
    ppermute x1 -> x2, waiting for transfers between devices: 12.4 us -> 4.64 us  [halves(): got[1:] = [lax.ppermute(piece, 'snap', [(0, 1)]) for piece in got[1:]]]
    pallas_call x1, Pallas kernels: 55 us -> 59.1 us  [partial_grams(): pl.pallas_call(functools.partial(partial_kernel, pieces), name='partial_g...]
    ppermute x1 -> x2, starting transfers between devices: 2.63 us -> 5.32 us  [halves(): got[1:] = [lax.ppermute(piece, 'snap', [(0, 1)]) for piece in got[1:]]]
    pallas_call x2 -> x3, Pallas kernels: 3.32 us -> 4.21 us  [form_basis(): pl.pallas_call(functools.partial(basis_kernel, pieces, start), name='form...]
  transfers between devices with their start and end apart: 1 -> 2, of which waited for: 1 -> 1; matrix products, arithmetic and copies ran while one was open for 0% -> 0% of each run, Pallas kernels for 29% -> 30%
where the time goes in v3:
time: 104 us
  Pallas kernels  91.9 us (88%)
  starting transfers between devices  5.32 us (5%)
  waiting for transfers between devices  4.64 us (4%)
  between operations  1.36 us (1%)
    pallas_call x1, Pallas kernels, partial_grams(): pl.pallas_call(functools.partial(partial_kernel, pieces), name='partial_g...  59.1 us
    pallas_call x1, Pallas kernels, reduce_rows(): pl.pallas_call(functools.partial(reduce_kernel, n), name='reduce_rows', o...  15.9 us
    pallas_call x1, Pallas kernels, factor(): pl.pallas_call(functools.partial(factor_kernel, scale), name='factor', ou...  12.6 us
    ppermute x2, starting transfers between devices, halves(): got[1:] = [lax.ppermute(piece, 'snap', [(0, 1)]) for piece in got[1:]]  5.32 us
    ppermute x2, waiting for transfers between devices, halves(): got[1:] = [lax.ppermute(piece, 'snap', [(0, 1)]) for piece in got[1:]]  4.64 us
    pallas_call x3, Pallas kernels, form_basis(): pl.pallas_call(functools.partial(basis_kernel, pieces, start), name='form...  4.21 us
  transfers between devices with their start and end apart: 2, of which 1 were waited for; matrix products, arithmetic and copies ran while one was open for 0% of the time, Pallas kernels for 30%

profile of v3, /device:TPU:0, one launch (start us, length us, event | category | flops | bytes accessed | tf_op | source)
XLA Modules:
  0.0 104.1 jit_solution(17086596585701338412)
XLA Ops:
  1.3 59.1 %partial_grams.1 = (f32[384,128]{1,0:T(8,128)}, bf16[128,9216]{1,0:T(8,128)(2,1)}, bf16[128,5120]{1,0:T(8,128)(2,1)}, bf16[128,2048]{1,0:T(8,128)(2,1)}) custom-call(s32[1]{0:T(128)S(6)} %copy.8.counts_ref, bf16[128,16384]{1,0:T(8,128)(2,1)} %own_ref.5), custom_call_target="tpu_custom_call" | custom-call | tf_op jit(solution)/shard_map/partial_grams/pallas_call | solution.py:182
  60.4 0.0 copy-start
  60.4 0.0 copy-start.1
  60.4 3.9 %collective-permute-start.1 = (bf16[128,5120]{1,0:T(8,128)(2,1)}, bf16[128,5120]{1,0:T(8,128)(2,1)S(1)}, u32[]{:S(2)}, u32[]{:S(2)}) collective-permute-start(bf16[128,5120]{1,0:T(8,128)(2,1)} %get-tuple-element.13), channel_id=1, source_target_pairs={{0,16},{1,17},{2,18},{3,19},{4,20},{5,21},{6,22},{7,23},{8,24},{9,... | collective-permute-start | bytes 3932168 | tf_op jit(solution)/shard_map/ppermute | solution.py:468
  64.4 1.4 %collective-permute-start = (bf16[128,2048]{1,0:T(8,128)(2,1)}, bf16[128,2048]{1,0:T(8,128)(2,1)S(1)}, u32[]{:S(2)}, u32[]{:S(2)}) collective-permute-start(bf16[128,2048]{1,0:T(8,128)(2,1)} %get-tuple-element.12), channel_id=1, source_target_pairs={{0,16},{1,17},{2,18},{3,19},{4,20},{5,21},{6,22},{7,23},{8,24},{9,... | collective-permute-start | bytes 1572872 | tf_op jit(solution)/shard_map/ppermute | solution.py:468
  65.8 0.0 copy-start.2
  65.8 0.9 copy-done.2
  66.7 15.9 %reduce_rows.1.gram_ref = f32[384,128]{1,0:T(8,128)S(1)} custom-call(f32[384,128]{1,0:T(8,128)S(1)} %copy-done.2), custom_call_target="tpu_custom_call" | custom-call | flops 1073741824 | bytes 50331648 | tf_op jit(solution)/shard_map/reduce_rows/pallas_call | solution.py:268
  82.6 12.6 %factor.1 = (f32[256,256]{1,0:T(8,128)}, bf16[128,128]{1,0:T(8,128)(2,1)S(1)}, bf16[128,128]{1,0:T(8,128)(2,1)S(1)}) custom-call(f32[384,128]{1,0:T(8,128)S(1)} %reduce_rows.1.gram_ref), custom_call_target="tpu_custom_call" | custom-call | flops 1073741824 | bytes 100663296 | tf_op jit(solution)/shard_map/factor/pallas_call | solution.py:382
  95.2 0.0 copy-done
  95.2 0.0 copy-done.1
  95.2 1.7 %form_basis.3.rest_0_ = bf16[128,16384]{1,0:T(8,128)(2,1)} custom-call(s32[1]{0:T(128)S(6)} %copy.8.counts_ref, bf16[128,128]{1,0:T(8,128)(2,1)S(1)} %get-tuple-element.10.own_w, bf16[128,128]{1,0:T(8,128)(2,1)S(1)} %get-tuple-element.11.other_w, bf16[128,16384]{1,0:T(8,128)(2,1)S(1)} %copy-done, bf16[128,9216]{1,0:T(8,128)(2,1)S(1)} %copy-done.1), custom_call_target="tpu_custom_call" | custom-call | flops 603979776 | bytes 9437184 | tf_op jit(solution)/shard_map/form_basis/pallas_call | solution.py:444
  97.0 0.0 collective-permute-done.1.got_ref
  97.0 1.4 %form_basis.4.rest_0_ = bf16[128,16384]{1,0:T(8,128)(2,1)} custom-call(s32[1]{0:T(128)S(6)} %copy.8.counts_ref, bf16[128,128]{1,0:T(8,128)(2,1)S(1)} %get-tuple-element.10.own_w, bf16[128,128]{1,0:T(8,128)(2,1)S(1)} %get-tuple-element.11.other_w, bf16[128,16384]{1,0:T(8,128)(2,1)S(1)} %copy-done, ...), custom_call_target="tpu_custom_call", output_to_operand_aliasing={{}: (5, {})} | custom-call | flops 335544320 | bytes 5242880 | tf_op jit(solution)/shard_map/form_basis/pallas_call | solution.py:444
  98.4 4.6 %collective-permute-done.got_ref = bf16[128,2048]{1,0:T(8,128)(2,1)S(1)} collective-permute-done((bf16[128,2048]{1,0:T(8,128)(2,1)}, bf16[128,2048]{1,0:T(8,128)(2,1)S(1)}, u32[]{:S(2)}, u32[]{:S(2)}) %collective-permute-start) | collective-permute-done | bytes 524320 | tf_op jit(solution)/shard_map/ppermute | solution.py:468
  103.0 1.1 %form_basis.5 = bf16[128,16384]{1,0:T(8,128)(2,1)} custom-call(s32[1]{0:T(128)S(6)} %copy.8.counts_ref, bf16[128,128]{1,0:T(8,128)(2,1)S(1)} %get-tuple-element.10.own_w, bf16[128,128]{1,0:T(8,128)(2,1)S(1)} %get-tuple-element.11.other_w, bf16[128,16384]{1,0:T(8,128)(2,1)S(1)} %copy-done, ...), custom_call_target="tpu_custom_call", output_to_operand_aliasing={{}: (5, {})} | custom-call | flops 134217728 | bytes 2097152 | tf_op jit(solution)/shard_map/form_basis/pallas_call | solution.py:444
Async XLA Ops:
  60.4 34.8 %copy-start = (bf16[128,16384]{1,0:T(8,128)(2,1)S(1)}, bf16[128,16384]{1,0:T(8,128)(2,1)}, u32[]{:S(2)}) copy-start(bf16[128,16384]{1,0:T(8,128)(2,1)} %own_ref.5) | copy-start | bytes 12582916
  60.4 34.8 %copy-start.1 = (bf16[128,9216]{1,0:T(8,128)(2,1)S(1)}, bf16[128,9216]{1,0:T(8,128)(2,1)}, u32[]{:S(2)}) copy-start(bf16[128,9216]{1,0:T(8,128)(2,1)} %get-tuple-element.14.got_ref) | copy-start | bytes 7077892
  60.4 36.6 %collective-permute-start.1 = (bf16[128,5120]{1,0:T(8,128)(2,1)}, bf16[128,5120]{1,0:T(8,128)(2,1)S(1)}, u32[]{:S(2)}, u32[]{:S(2)}) collective-permute-start(bf16[128,5120]{1,0:T(8,128)(2,1)} %get-tuple-element.13), channel_id=1, source_target_pairs={{0,16},{1,17},{2,18},{3,19},{4,20},{5,21},{6,22},{7,23},{8,24},{9,... | collective-permute-start | bytes 3932168 | tf_op jit(solution)/shard_map/ppermute | solution.py:468
  64.4 38.6 %collective-permute-start = (bf16[128,2048]{1,0:T(8,128)(2,1)}, bf16[128,2048]{1,0:T(8,128)(2,1)S(1)}, u32[]{:S(2)}, u32[]{:S(2)}) collective-permute-start(bf16[128,2048]{1,0:T(8,128)(2,1)} %get-tuple-element.12), channel_id=1, source_target_pairs={{0,16},{1,17},{2,18},{3,19},{4,20},{5,21},{6,22},{7,23},{8,24},{9,... | collective-permute-start | bytes 1572872 | tf_op jit(solution)/shard_map/ppermute | solution.py:468
  65.8 0.9 copy-start.2

commit v4 on v3

--- a/solution.py
+++ b/solution.py
@@ -59,11 +59,13 @@
 
 def partial_kernel(
     pieces, counts_ref, x_ref, part_ref, first_ref, later_ref, last_ref,
-    own, got, mine, theirs,
-    load_sem, send_sem, recv_sem, keep_sem, back_sem, sum_send, sum_recv,
+    own, got, mine, near, summed, theirs,
+    load_sem, send_sem, recv_sem, keep_sem, back_sem, sum_send, sum_recv, near_send, near_recv,
 ):
     snap = lax.axis_index("snap")
+    core = lax.rem(lax.axis_index("row"), 2)
     other = {"snap": 1 - snap}
+    pair = {"row": lax.axis_index("row") + 1 - 2 * core}
     narrow, slots = x_ref.shape
     half = slots // 2
     step = half // pieces
@@ -71,6 +73,7 @@
 
     barrier = pltpu.get_barrier_semaphore()
     pl.semaphore_signal(barrier, inc=1, device_id=other, device_id_type=MESH)
+    pl.semaphore_signal(barrier, inc=1, device_id=pair, device_id_type=MESH)
 
     loads = []
     for c in range(2 * pieces):
@@ -79,7 +82,7 @@
         copy.start()
         loads.append(copy)
 
-    pl.semaphore_wait(barrier, 1)
+    pl.semaphore_wait(barrier, 2)
 
     def send(i, src, dst, size):
         copy = pltpu.make_async_remote_copy(
@@ -117,9 +120,23 @@
         keeps.append(keep)
         start += size
 
+    rows = narrow // 2
+
     def sum_copy(i):
+        away = pltpu.make_async_remote_copy(
+            src_ref=mine.at[i, pl.ds(pl.multiple_of((1 - core) * rows, SUBLANES), rows)],
+            dst_ref=near.at[i],
+            send_sem=near_send.at[i],
+            recv_sem=near_recv.at[i],
+            device_id=pair,
+            device_id_type=MESH,
+        )
+        away.start()
+        away.wait()
+        kept = mine[i, pl.ds(pl.multiple_of(core * rows, SUBLANES), rows), :]
+        summed[i] = kept + near[i]
         return pltpu.make_async_remote_copy(
-            src_ref=mine.at[i],
+            src_ref=summed.at[i],
             dst_ref=theirs.at[i],
             send_sem=sum_send.at[i],
             recv_sem=sum_recv.at[i],
@@ -129,7 +146,8 @@
 
     diagonal = sum_copy(0)
     diagonal.start()
-    ahead = (first_ref.shape[1] - half) // 2
+    spare = first_ref.shape[1] - half
+    ahead = spare * 3 // 4
     extras = [send(pieces, half, half, ahead)]
 
     cross = jnp.zeros((narrow, narrow), jnp.float32)
@@ -147,21 +165,21 @@
     mine[1] = jnp.where(snap == 0, cross, cross.T)
     crossed = sum_copy(1)
     crossed.start()
-    extras.append(send(pieces + 1, half + ahead, half + ahead, ahead))
+    extras.append(send(pieces + 1, half + ahead, half + ahead, spare - ahead))
     for copy in sends:
         copy.wait_send()
     for copy in keeps:
         copy.wait()
     diagonal.wait()
-    low = jnp.where(snap == 0, mine[0], theirs[0])
-    high = jnp.where(snap == 0, theirs[0], mine[0])
-    part_ref[0:narrow, :] = low
-    part_ref[narrow:2 * narrow, :] = high
+    part_ref[0:rows, :] = jnp.where(snap == 0, summed[0], theirs[0])
+    part_ref[rows:2 * rows, :] = jnp.where(snap == 0, theirs[0], summed[0])
     crossed.wait()
-    part_ref[2 * narrow:3 * narrow, :] = mine[1] + theirs[1]
-    for i, copy in enumerate(extras):
+    part_ref[2 * rows:3 * rows, :] = summed[1] + theirs[1]
+    for i, (copy, at, size) in enumerate(
+        zip(extras, (half, half + ahead), (ahead, spare - ahead))
+    ):
         copy.wait()
-        here = pl.ds(half + i * ahead, ahead)
+        here = pl.ds(at, size)
         back = pltpu.make_async_copy(
             got.at[:, here], first_ref.at[:, here], back_sem.at[pieces + i]
         )
@@ -183,7 +201,7 @@
         functools.partial(partial_kernel, pieces),
         name="partial_grams",
         out_shape=(
-            jax.ShapeDtypeStruct((3 * narrow, narrow), jnp.float32),
+            jax.ShapeDtypeStruct((3 * narrow // 2, narrow), jnp.float32),
             jax.ShapeDtypeStruct((narrow, early), snapshots.dtype),
             jax.ShapeDtypeStruct((narrow, later), snapshots.dtype),
             jax.ShapeDtypeStruct((narrow, last), snapshots.dtype),
@@ -197,7 +215,9 @@
             pltpu.VMEM((narrow, slots), snapshots.dtype),
             pltpu.VMEM((narrow, early), snapshots.dtype),
             pltpu.VMEM((2, narrow, narrow), jnp.float32),
-            pltpu.VMEM((2, narrow, narrow), jnp.float32),
+            pltpu.VMEM((2, narrow // 2, narrow), jnp.float32),
+            pltpu.VMEM((2, narrow // 2, narrow), jnp.float32),
+            pltpu.VMEM((2, narrow // 2, narrow), jnp.float32),
             pltpu.SemaphoreType.DMA((2 * pieces,)),
             pltpu.SemaphoreType.DMA((pieces + 2,)),
             pltpu.SemaphoreType.DMA((pieces + 2,)),
@@ -205,6 +225,8 @@
             pltpu.SemaphoreType.DMA((pieces + 2,)),
             pltpu.SemaphoreType.DMA((2,)),
             pltpu.SemaphoreType.DMA((2,)),
+            pltpu.SemaphoreType.DMA((2,)),
+            pltpu.SemaphoreType.DMA((2,)),
         ],
         compiler_params=pltpu.CompilerParams(
             collective_id=0, has_side_effects=True, vmem_limit_bytes=62 << 20
@@ -214,7 +236,9 @@
 
 def reduce_kernel(n, part_ref, out_ref, parts, send_sem, recv_sem, out_send, out_recv):
     me = lax.axis_index("row")
-    rows = part_ref.shape[0] // n
+    core, chip = lax.rem(me, 2), lax.div(me, 2)
+    chips = n // 2
+    rows = part_ref.shape[0] // chips
     barrier = pltpu.get_barrier_semaphore()
     for d in range(1, n):
         peer = lax.rem(me + d, n)
@@ -225,29 +249,29 @@
         return pl.ds(pl.multiple_of(i * rows, SUBLANES), rows)
 
     copies = []
-    for d in range(1, n):
-        peer = lax.rem(me + d, n)
+    for d in range(1, chips):
+        peer = lax.rem(chip + d, chips)
         copy = pltpu.make_async_remote_copy(
             src_ref=part_ref.at[at(peer)],
             dst_ref=parts.at[d - 1],
             send_sem=send_sem.at[d - 1],
             recv_sem=recv_sem.at[d - 1],
-            device_id={"row": peer},
+            device_id={"row": 2 * peer + core},
             device_id_type=MESH,
         )
         copy.start()
         copies.append(copy)
-    total = part_ref[at(me), :]
-    for d in range(1, n):
+    total = part_ref[at(chip), :]
+    for d in range(1, chips):
         copies[d - 1].wait_recv()
         total = total + parts[d - 1]
-    out_ref[at(me), :] = total
+    out_ref[core, at(chip), :] = total
     results = []
     for d in range(1, n):
         peer = lax.rem(me + d, n)
         copy = pltpu.make_async_remote_copy(
-            src_ref=out_ref.at[at(me)],
-            dst_ref=out_ref.at[at(me)],
+            src_ref=out_ref.at[core, at(chip)],
+            dst_ref=out_ref.at[core, at(chip)],
             send_sem=out_send.at[d - 1],
             recv_sem=out_recv.at[d - 1],
             device_id={"row": peer},
@@ -263,18 +287,19 @@
 
 def reduce_rows(part):
     n = lax.axis_size("row")
-    rows = part.shape[0] // n
+    chips = n // 2
+    rows = part.shape[0] // chips
     vmem = pl.BlockSpec(memory_space=pltpu.VMEM)
     return pl.pallas_call(
         functools.partial(reduce_kernel, n),
         name="reduce_rows",
-        out_shape=jax.ShapeDtypeStruct(part.shape, part.dtype),
+        out_shape=jax.ShapeDtypeStruct((2, *part.shape), part.dtype),
         in_specs=[vmem],
         out_specs=vmem,
         scratch_shapes=[
-            pltpu.VMEM((n - 1, rows, part.shape[1]), part.dtype),
-            pltpu.SemaphoreType.DMA((n - 1,)),
-            pltpu.SemaphoreType.DMA((n - 1,)),
+            pltpu.VMEM((chips - 1, rows, part.shape[1]), part.dtype),
+            pltpu.SemaphoreType.DMA((chips - 1,)),
+            pltpu.SemaphoreType.DMA((chips - 1,)),
             pltpu.SemaphoreType.DMA((n - 1,)),
             pltpu.SemaphoreType.DMA((n - 1,)),
         ],
@@ -327,10 +352,15 @@
 
 
 def factor_kernel(scale, gram_ref, r_ref, own_ref, other_ref, work, roots):
-    narrow = gram_ref.shape[1]
+    narrow = gram_ref.shape[2]
+    rows = narrow // 2
     snap = lax.axis_index("snap")
     row = lax.broadcasted_iota(jnp.int32, (narrow, narrow), 0)
     col = lax.broadcasted_iota(jnp.int32, (narrow, narrow), 1)
+
+    def gram(i):
+        here = slice(i * rows, (i + 1) * rows)
+        return jnp.concatenate([gram_ref[0, here, :], gram_ref[1, here, :]], axis=0)
 
     def dot(a, b, dims):
         return lax.dot_general(
@@ -344,8 +374,8 @@
         upper = jnp.where(col == row, 1.0 / full, upper)
         return inverse, upper
 
-    work[0] = gram_ref[0:narrow, :]
-    work[1] = gram_ref[narrow:2 * narrow, :]
+    work[0] = gram(0)
+    work[1] = gram(1)
 
     @pl.loop(0, 2)
     def _(block):
@@ -358,7 +388,7 @@
         @pl.when(block == 0)
         def _():
             inverse, _ = diagonal(0)
-            right = dot(inverse, gram_ref[2 * narrow:3 * narrow, :], ((1,), (0,)))
+            right = dot(inverse, gram(2), ((1,), (0,)))
             roots[...] = right
             work[1] = work[1] - dot(right, right, ((0,), (0,)))
 
@@ -377,7 +407,7 @@
 
 
 def factor(gram, scale, dtype):
-    narrow = gram.shape[1]
+    narrow = gram.shape[2]
     vmem = pl.BlockSpec(memory_space=pltpu.VMEM)
     return pl.pallas_call(
         functools.partial(factor_kernel, scale),

time: 104 us -> 103 us (level)
  Pallas kernels: 91.9 us -> 89.2 us
  waiting for transfers between devices: 4.64 us -> 6.68 us
    ppermute x2, waiting for transfers between devices: 4.64 us -> 6.68 us  [halves(): got[1:] = [lax.ppermute(piece, 'snap', [(0, 1)]) for piece in got[1:]]]
    pallas_call x1, Pallas kernels: 15.9 us -> 14.1 us  [reduce_rows(): pl.pallas_call(functools.partial(reduce_kernel, n), name='reduce_rows', o...]
  transfers between devices with their start and end apart: 2 -> 2, of which waited for: 1 -> 1; matrix products, arithmetic and copies ran while one was open for 0% -> 0% of each run, Pallas kernels for 30% -> 29%
where the time goes in v4:
time: 103 us
  Pallas kernels  89.2 us (87%)
  waiting for transfers between devices  6.68 us (6%)
  starting transfers between devices  4.69 us (5%)
  between operations  1.36 us (1%)
    pallas_call x1, Pallas kernels, partial_grams(): pl.pallas_call(functools.partial(partial_kernel, pieces), name='partial_g...  58.3 us
    pallas_call x1, Pallas kernels, reduce_rows(): pl.pallas_call(functools.partial(reduce_kernel, n), name='reduce_rows', o...  14.1 us
    pallas_call x1, Pallas kernels, factor(): pl.pallas_call(functools.partial(factor_kernel, scale), name='factor', ou...  12.6 us
    ppermute x2, waiting for transfers between devices, halves(): got[1:] = [lax.ppermute(piece, 'snap', [(0, 1)]) for piece in got[1:]]  6.68 us
    ppermute x2, starting transfers between devices, halves(): got[1:] = [lax.ppermute(piece, 'snap', [(0, 1)]) for piece in got[1:]]  4.69 us
    pallas_call x3, Pallas kernels, form_basis(): pl.pallas_call(functools.partial(basis_kernel, pieces, start), name='form...  4.21 us
  transfers between devices with their start and end apart: 2, of which 1 were waited for; matrix products, arithmetic and copies ran while one was open for 0% of the time, Pallas kernels for 29%

profile of v4, /device:TPU:0, one launch (start us, length us, event | category | flops | bytes accessed | tf_op | source)
XLA Modules:
  0.0 102.8 jit_solution(17414535040604060718)
XLA Ops:
  1.3 58.3 %partial_grams.1 = (f32[192,128]{1,0:T(8,128)}, bf16[128,9216]{1,0:T(8,128)(2,1)}, bf16[128,5120]{1,0:T(8,128)(2,1)}, bf16[128,2048]{1,0:T(8,128)(2,1)}) custom-call(s32[1]{0:T(128)S(6)} %copy.8.counts_ref, bf16[128,16384]{1,0:T(8,128)(2,1)} %own_ref.5), custom_call_target="tpu_custom_call" | custom-call | tf_op jit(solution)/shard_map/partial_grams/pallas_call | solution.py:200
  59.6 0.0 copy-start
  59.6 0.0 copy-start.1
  59.6 3.3 %collective-permute-start.1 = (bf16[128,5120]{1,0:T(8,128)(2,1)}, bf16[128,5120]{1,0:T(8,128)(2,1)S(1)}, u32[]{:S(2)}, u32[]{:S(2)}) collective-permute-start(bf16[128,5120]{1,0:T(8,128)(2,1)} %get-tuple-element.13), channel_id=1, source_target_pairs={{0,16},{1,17},{2,18},{3,19},{4,20},{5,21},{6,22},{7,23},{8,24},{9,... | collective-permute-start | bytes 3932168 | tf_op jit(solution)/shard_map/ppermute | solution.py:498
  62.9 1.4 %collective-permute-start = (bf16[128,2048]{1,0:T(8,128)(2,1)}, bf16[128,2048]{1,0:T(8,128)(2,1)S(1)}, u32[]{:S(2)}, u32[]{:S(2)}) collective-permute-start(bf16[128,2048]{1,0:T(8,128)(2,1)} %get-tuple-element.12), channel_id=1, source_target_pairs={{0,16},{1,17},{2,18},{3,19},{4,20},{5,21},{6,22},{7,23},{8,24},{9,... | collective-permute-start | bytes 1572872 | tf_op jit(solution)/shard_map/ppermute | solution.py:498
  64.3 0.0 copy-start.2
  64.3 0.9 copy-done.2
  65.2 14.1 %reduce_rows.1.gram_ref = f32[2,192,128]{2,1,0:T(8,128)S(1)} custom-call(f32[192,128]{1,0:T(8,128)S(1)} %copy-done.2), custom_call_target="tpu_custom_call" | custom-call | flops 1073741824 | bytes 50331648 | tf_op jit(solution)/shard_map/reduce_rows/pallas_call | solution.py:293
  79.3 12.6 %factor.1 = (f32[256,256]{1,0:T(8,128)}, bf16[128,128]{1,0:T(8,128)(2,1)S(1)}, bf16[128,128]{1,0:T(8,128)(2,1)S(1)}) custom-call(f32[2,192,128]{2,1,0:T(8,128)S(1)} %reduce_rows.1.gram_ref), custom_call_target="tpu_custom_call" | custom-call | flops 1073741824 | bytes 100663296 | tf_op jit(solution)/shard_map/factor/pallas_call | solution.py:412
  91.9 0.0 copy-done
  91.9 0.0 copy-done.1
  91.9 1.7 %form_basis.3.rest_0_ = bf16[128,16384]{1,0:T(8,128)(2,1)} custom-call(s32[1]{0:T(128)S(6)} %copy.8.counts_ref, bf16[128,128]{1,0:T(8,128)(2,1)S(1)} %get-tuple-element.10.own_w, bf16[128,128]{1,0:T(8,128)(2,1)S(1)} %get-tuple-element.11.other_w, bf16[128,16384]{1,0:T(8,128)(2,1)S(1)} %copy-done, bf16[128,9216]{1,0:T(8,128)(2,1)S(1)} %copy-done.1), custom_call_target="tpu_custom_call" | custom-call | flops 603979776 | bytes 9437184 | tf_op jit(solution)/shard_map/form_basis/pallas_call | solution.py:474
  93.6 0.0 collective-permute-done.1.got_ref
  93.6 1.4 %form_basis.4.rest_0_ = bf16[128,16384]{1,0:T(8,128)(2,1)} custom-call(s32[1]{0:T(128)S(6)} %copy.8.counts_ref, bf16[128,128]{1,0:T(8,128)(2,1)S(1)} %get-tuple-element.10.own_w, bf16[128,128]{1,0:T(8,128)(2,1)S(1)} %get-tuple-element.11.other_w, bf16[128,16384]{1,0:T(8,128)(2,1)S(1)} %copy-done, ...), custom_call_target="tpu_custom_call", output_to_operand_aliasing={{}: (5, {})} | custom-call | flops 335544320 | bytes 5242880 | tf_op jit(solution)/shard_map/form_basis/pallas_call | solution.py:474
  95.0 6.7 %collective-permute-done.got_ref = bf16[128,2048]{1,0:T(8,128)(2,1)S(1)} collective-permute-done((bf16[128,2048]{1,0:T(8,128)(2,1)}, bf16[128,2048]{1,0:T(8,128)(2,1)S(1)}, u32[]{:S(2)}, u32[]{:S(2)}) %collective-permute-start) | collective-permute-done | bytes 524320 | tf_op jit(solution)/shard_map/ppermute | solution.py:498
  101.7 1.1 %form_basis.5 = bf16[128,16384]{1,0:T(8,128)(2,1)} custom-call(s32[1]{0:T(128)S(6)} %copy.8.counts_ref, bf16[128,128]{1,0:T(8,128)(2,1)S(1)} %get-tuple-element.10.own_w, bf16[128,128]{1,0:T(8,128)(2,1)S(1)} %get-tuple-element.11.other_w, bf16[128,16384]{1,0:T(8,128)(2,1)S(1)} %copy-done, ...), custom_call_target="tpu_custom_call", output_to_operand_aliasing={{}: (5, {})} | custom-call | flops 134217728 | bytes 2097152 | tf_op jit(solution)/shard_map/form_basis/pallas_call | solution.py:474
Async XLA Ops:
  59.6 32.3 %copy-start = (bf16[128,16384]{1,0:T(8,128)(2,1)S(1)}, bf16[128,16384]{1,0:T(8,128)(2,1)}, u32[]{:S(2)}) copy-start(bf16[128,16384]{1,0:T(8,128)(2,1)} %own_ref.5) | copy-start | bytes 12582916
  59.6 32.3 %copy-start.1 = (bf16[128,9216]{1,0:T(8,128)(2,1)S(1)}, bf16[128,9216]{1,0:T(8,128)(2,1)}, u32[]{:S(2)}) copy-start(bf16[128,9216]{1,0:T(8,128)(2,1)} %get-tuple-element.14.got_ref) | copy-start | bytes 7077892
  59.6 34.0 %collective-permute-start.1 = (bf16[128,5120]{1,0:T(8,128)(2,1)}, bf16[128,5120]{1,0:T(8,128)(2,1)S(1)}, u32[]{:S(2)}, u32[]{:S(2)}) collective-permute-start(bf16[128,5120]{1,0:T(8,128)(2,1)} %get-tuple-element.13), channel_id=1, source_target_pairs={{0,16},{1,17},{2,18},{3,19},{4,20},{5,21},{6,22},{7,23},{8,24},{9,... | collective-permute-start | bytes 3932168 | tf_op jit(solution)/shard_map/ppermute | solution.py:498
  62.9 38.8 %collective-permute-start = (bf16[128,2048]{1,0:T(8,128)(2,1)}, bf16[128,2048]{1,0:T(8,128)(2,1)S(1)}, u32[]{:S(2)}, u32[]{:S(2)}) collective-permute-start(bf16[128,2048]{1,0:T(8,128)(2,1)} %get-tuple-element.12), channel_id=1, source_target_pairs={{0,16},{1,17},{2,18},{3,19},{4,20},{5,21},{6,22},{7,23},{8,24},{9,... | collective-permute-start | bytes 1572872 | tf_op jit(solution)/shard_map/ppermute | solution.py:498
  64.3 0.9 copy-start.2

commit v5 on v4

--- a/solution.py
+++ b/solution.py
@@ -84,10 +84,10 @@
 
     pl.semaphore_wait(barrier, 2)
 
-    def send(i, src, dst, size):
+    def send(i, src, into, dst, size):
         copy = pltpu.make_async_remote_copy(
             src_ref=x_ref.at[:, pl.ds(src, size)],
-            dst_ref=got.at[:, pl.ds(dst, size)],
+            dst_ref=into.at[:, pl.ds(dst, size)],
             send_sem=send_sem.at[i],
             recv_sem=recv_sem.at[i],
             device_id=other,
@@ -97,7 +97,7 @@
         return copy
 
     sends = [
-        send(c, pl.multiple_of(snap * half + c * step, step), c * step, step)
+        send(c, pl.multiple_of(snap * half + c * step, step), got, c * step, step)
         for c in range(pieces)
     ]
 
@@ -148,7 +148,7 @@
     diagonal.start()
     spare = first_ref.shape[1] - half
     ahead = spare * 3 // 4
-    extras = [send(pieces, half, half, ahead)]
+    extras = [send(pieces, half, first_ref, half, ahead)]
 
     cross = jnp.zeros((narrow, narrow), jnp.float32)
     backs = []
@@ -165,7 +165,8 @@
     mine[1] = jnp.where(snap == 0, cross, cross.T)
     crossed = sum_copy(1)
     crossed.start()
-    extras.append(send(pieces + 1, half + ahead, half + ahead, spare - ahead))
+    at = half + ahead
+    extras.append(send(pieces + 1, at, first_ref, at, spare - ahead))
     for copy in sends:
         copy.wait_send()
     for copy in keeps:
@@ -175,16 +176,8 @@
     part_ref[rows:2 * rows, :] = jnp.where(snap == 0, theirs[0], summed[0])
     crossed.wait()
     part_ref[2 * rows:3 * rows, :] = summed[1] + theirs[1]
-    for i, (copy, at, size) in enumerate(
-        zip(extras, (half, half + ahead), (ahead, spare - ahead))
-    ):
+    for copy in extras:
         copy.wait()
-        here = pl.ds(at, size)
-        back = pltpu.make_async_copy(
-            got.at[:, here], first_ref.at[:, here], back_sem.at[pieces + i]
-        )
-        back.start()
-        backs.append(back)
     for copy in backs:
         copy.wait()
 
@@ -194,7 +187,7 @@
     half = slots // 2
     step = half // pieces
     early = half + step
-    last = 2 * step
+    last = step
     later = slots - early - last
     any_space = pl.BlockSpec(memory_space=pl.ANY)
     return pl.pallas_call(
@@ -213,7 +206,7 @@
         out_specs=(pl.BlockSpec(memory_space=pltpu.VMEM), any_space, any_space, any_space),
         scratch_shapes=[
             pltpu.VMEM((narrow, slots), snapshots.dtype),
-            pltpu.VMEM((narrow, early), snapshots.dtype),
+            pltpu.VMEM((narrow, half), snapshots.dtype),
             pltpu.VMEM((2, narrow, narrow), jnp.float32),
             pltpu.VMEM((2, narrow // 2, narrow), jnp.float32),
             pltpu.VMEM((2, narrow // 2, narrow), jnp.float32),
@@ -222,7 +215,7 @@
             pltpu.SemaphoreType.DMA((pieces + 2,)),
             pltpu.SemaphoreType.DMA((pieces + 2,)),
             pltpu.SemaphoreType.DMA((2,)),
-            pltpu.SemaphoreType.DMA((pieces + 2,)),
+            pltpu.SemaphoreType.DMA((pieces,)),
             pltpu.SemaphoreType.DMA((2,)),
             pltpu.SemaphoreType.DMA((2,)),
             pltpu.SemaphoreType.DMA((2,)),

time: 103 us -> 102 us (level)
  transfers between devices with their start and end apart: 2 -> 2, of which waited for: 1 -> 2; matrix products, arithmetic and copies ran while one was open for 0% -> 0% of each run, Pallas kernels for 29% -> 29%
where the time goes in v5:
time: 102 us
  Pallas kernels  88.6 us (87%)
  waiting for transfers between devices  6.6 us (6%)
  starting transfers between devices  4.67 us (5%)
  between operations  1.35 us (1%)
    pallas_call x1, Pallas kernels, partial_grams(): pl.pallas_call(functools.partial(partial_kernel, pieces), name='partial_g...  57.8 us
    pallas_call x1, Pallas kernels, reduce_rows(): pl.pallas_call(functools.partial(reduce_kernel, n), name='reduce_rows', o...  14.1 us
    pallas_call x1, Pallas kernels, factor(): pl.pallas_call(functools.partial(factor_kernel, scale), name='factor', ou...  12.6 us
    ppermute x2, waiting for transfers between devices, halves(): got[1:] = [lax.ppermute(piece, 'snap', [(0, 1)]) for piece in got[1:]]  6.6 us
    ppermute x2, starting transfers between devices, halves(): got[1:] = [lax.ppermute(piece, 'snap', [(0, 1)]) for piece in got[1:]]  4.67 us
    pallas_call x3, Pallas kernels, form_basis(): pl.pallas_call(functools.partial(basis_kernel, pieces, start), name='form...  4.15 us
  transfers between devices with their start and end apart: 2, of which 2 were waited for; matrix products, arithmetic and copies ran while one was open for 0% of the time, Pallas kernels for 29%

profile of v5, /device:TPU:0, one launch (start us, length us, event | category | flops | bytes accessed | tf_op | source)
XLA Modules:
  0.0 102.1 jit_solution(7937529208775337382)
XLA Ops:
  1.3 57.8 %partial_grams.1 = (f32[192,128]{1,0:T(8,128)}, bf16[128,9216]{1,0:T(8,128)(2,1)}, bf16[128,6144]{1,0:T(8,128)(2,1)}, bf16[128,1024]{1,0:T(8,128)(2,1)}) custom-call(s32[1]{0:T(128)S(6)} %copy.8.counts_ref, bf16[128,16384]{1,0:T(8,128)(2,1)} %own_ref.5), custom_call_target="tpu_custom_call" | custom-call | tf_op jit(solution)/shard_map/partial_grams/pallas_call | solution.py:193
  59.1 0.0 copy-start
  59.1 0.0 copy-start.1
  59.1 3.3 %collective-permute-start.1 = (bf16[128,6144]{1,0:T(8,128)(2,1)}, bf16[128,6144]{1,0:T(8,128)(2,1)S(1)}, u32[]{:S(2)}, u32[]{:S(2)}) collective-permute-start(bf16[128,6144]{1,0:T(8,128)(2,1)} %get-tuple-element.13), channel_id=1, source_target_pairs={{0,16},{1,17},{2,18},{3,19},{4,20},{5,21},{6,22},{7,23},{8,24},{9,... | collective-permute-start | bytes 4718600 | tf_op jit(solution)/shard_map/ppermute | solution.py:491
  62.4 1.3 %collective-permute-start = (bf16[128,1024]{1,0:T(8,128)(2,1)}, bf16[128,1024]{1,0:T(8,128)(2,1)S(1)}, u32[]{:S(2)}, u32[]{:S(2)}) collective-permute-start(bf16[128,1024]{1,0:T(8,128)(2,1)} %get-tuple-element.12), channel_id=1, source_target_pairs={{0,16},{1,17},{2,18},{3,19},{4,20},{5,21},{6,22},{7,23},{8,24},{9,... | collective-permute-start | bytes 786440 | tf_op jit(solution)/shard_map/ppermute | solution.py:491
  63.8 0.0 copy-start.2
  63.8 0.9 copy-done.2
  64.7 14.1 %reduce_rows.1.gram_ref = f32[2,192,128]{2,1,0:T(8,128)S(1)} custom-call(f32[192,128]{1,0:T(8,128)S(1)} %copy-done.2), custom_call_target="tpu_custom_call" | custom-call | flops 1073741824 | bytes 50331648 | tf_op jit(solution)/shard_map/reduce_rows/pallas_call | solution.py:286
  78.7 12.6 %factor.1 = (f32[256,256]{1,0:T(8,128)}, bf16[128,128]{1,0:T(8,128)(2,1)S(1)}, bf16[128,128]{1,0:T(8,128)(2,1)S(1)}) custom-call(f32[2,192,128]{2,1,0:T(8,128)S(1)} %reduce_rows.1.gram_ref), custom_call_target="tpu_custom_call" | custom-call | flops 1073741824 | bytes 100663296 | tf_op jit(solution)/shard_map/factor/pallas_call | solution.py:405
  91.3 0.0 copy-done
  91.3 0.0 copy-done.1
  91.3 1.7 %form_basis.3.rest_0_ = bf16[128,16384]{1,0:T(8,128)(2,1)} custom-call(s32[1]{0:T(128)S(6)} %copy.8.counts_ref, bf16[128,128]{1,0:T(8,128)(2,1)S(1)} %get-tuple-element.10.own_w, bf16[128,128]{1,0:T(8,128)(2,1)S(1)} %get-tuple-element.11.other_w, bf16[128,16384]{1,0:T(8,128)(2,1)S(1)} %copy-done, bf16[128,9216]{1,0:T(8,128)(2,1)S(1)} %copy-done.1), custom_call_target="tpu_custom_call" | custom-call | flops 603979776 | bytes 9437184 | tf_op jit(solution)/shard_map/form_basis/pallas_call | solution.py:467
  93.1 4.3 %collective-permute-done.1.got_ref = bf16[128,6144]{1,0:T(8,128)(2,1)S(1)} collective-permute-done((bf16[128,6144]{1,0:T(8,128)(2,1)}, bf16[128,6144]{1,0:T(8,128)(2,1)S(1)}, u32[]{:S(2)}, u32[]{:S(2)}) %collective-permute-start.1) | collective-permute-done | bytes 1572896 | tf_op jit(solution)/shard_map/ppermute | solution.py:491
  97.4 1.5 %form_basis.4.rest_0_ = bf16[128,16384]{1,0:T(8,128)(2,1)} custom-call(s32[1]{0:T(128)S(6)} %copy.8.counts_ref, bf16[128,128]{1,0:T(8,128)(2,1)S(1)} %get-tuple-element.10.own_w, bf16[128,128]{1,0:T(8,128)(2,1)S(1)} %get-tuple-element.11.other_w, bf16[128,16384]{1,0:T(8,128)(2,1)S(1)} %copy-done, ...), custom_call_target="tpu_custom_call", output_to_operand_aliasing={{}: (5, {})} | custom-call | flops 402653184 | bytes 6291456 | tf_op jit(solution)/shard_map/form_basis/pallas_call | solution.py:467
  98.9 2.3 %collective-permute-done.got_ref = bf16[128,1024]{1,0:T(8,128)(2,1)S(1)} collective-permute-done((bf16[128,1024]{1,0:T(8,128)(2,1)}, bf16[128,1024]{1,0:T(8,128)(2,1)S(1)}, u32[]{:S(2)}, u32[]{:S(2)}) %collective-permute-start) | collective-permute-done | bytes 262176 | tf_op jit(solution)/shard_map/ppermute | solution.py:491
  101.2 0.9 form_basis.5
Async XLA Ops:
  59.1 32.3 %copy-start = (bf16[128,16384]{1,0:T(8,128)(2,1)S(1)}, bf16[128,16384]{1,0:T(8,128)(2,1)}, u32[]{:S(2)}) copy-start(bf16[128,16384]{1,0:T(8,128)(2,1)} %own_ref.5) | copy-start | bytes 12582916
  59.1 32.3 %copy-start.1 = (bf16[128,9216]{1,0:T(8,128)(2,1)S(1)}, bf16[128,9216]{1,0:T(8,128)(2,1)}, u32[]{:S(2)}) copy-start(bf16[128,9216]{1,0:T(8,128)(2,1)} %get-tuple-element.14.got_ref) | copy-start | bytes 7077892
  59.1 38.3 %collective-permute-start.1 = (bf16[128,6144]{1,0:T(8,128)(2,1)}, bf16[128,6144]{1,0:T(8,128)(2,1)S(1)}, u32[]{:S(2)}, u32[]{:S(2)}) collective-permute-start(bf16[128,6144]{1,0:T(8,128)(2,1)} %get-tuple-element.13), channel_id=1, source_target_pairs={{0,16},{1,17},{2,18},{3,19},{4,20},{5,21},{6,22},{7,23},{8,24},{9,... | collective-permute-start | bytes 4718600 | tf_op jit(solution)/shard_map/ppermute | solution.py:491
  62.4 38.7 %collective-permute-start = (bf16[128,1024]{1,0:T(8,128)(2,1)}, bf16[128,1024]{1,0:T(8,128)(2,1)S(1)}, u32[]{:S(2)}, u32[]{:S(2)}) collective-permute-start(bf16[128,1024]{1,0:T(8,128)(2,1)} %get-tuple-element.12), channel_id=1, source_target_pairs={{0,16},{1,17},{2,18},{3,19},{4,20},{5,21},{6,22},{7,23},{8,24},{9,... | collective-permute-start | bytes 786440 | tf_op jit(solution)/shard_map/ppermute | solution.py:491
  63.8 0.9 copy-start.2
